TPU v7x, 32 devices: a whole 2x2x4 slice. The times are simulated.
32 devices in a mesh: tm: 8 (over z, y), space: 4 (over x, core).
Axes of the slice: x: 2, y: 2, z: 4, core: 2. Of those that a mesh axis runs over, the one named last changes fastest.
Arguments:
- queries: bfloat16 [8, 16, 32, 768], P('tm', 'space')
- key_vectors: bfloat16 [8, 16, 32, 768], P('tm', 'space')
- values: bfloat16 [8, 16, 32, 768], P('tm', 'space'), may hold values from -6 to 6
- grad_out: bfloat16 [8, 16, 32, 768], P('tm', 'space'), may hold values from -6 to 6
- windows: int32 [2, 6], replicated, may hold values from 1 to 31, as said below
Outputs:
- attended: bfloat16 [8, 16, 32, 768], P('tm', 'space')
- grad_queries: bfloat16 [8, 16, 32, 768], P('tm', 'space')
- grad_keys: bfloat16 [8, 16, 32, 768], P('tm', 'space')
- value_gradient: bfloat16 [8, 16, 32, 768], P('tm', 'space')
Inputs may be any that keep to these rules, and one draw needn't show every extreme that they name: windows[0, h] is 1 to 2 and some head has 2; windows[1, h] is a quarter of 32 or more and some head has 31.
All inputs are finite; a program needn't handle non-finite values.
Results may differ from a plain program's by a relative error of at most 0.025.
Values may be sent and summed in bfloat16 or wider, within the bound.
A program may use at most 64 MiB of HBM per device.

v0:
```python
import functools
import math

import jax
import jax.numpy as jnp
from jax import lax
from jax.experimental import pallas as pl
from jax.experimental.pallas import tpu as pltpu
from jax.sharding import PartitionSpec as P

masked_score = -1e30
MESH = pl.DeviceIdType.MESH


def dot_nt(a, b):
    return lax.dot_general(a, b, (((1,), (1,)), ((), ())), preferred_element_type=jnp.float32)


def dot_nn(a, b):
    return lax.dot_general(a, b, (((1,), (0,)), ((), ())), preferred_element_type=jnp.float32)


def kernel(
    sizes,
    win_hbm,
    q_ref,
    k_ref,
    v_ref,
    g_ref,
    att_ref,
    gq_ref,
    gk_ref,
    gv_ref,
    win_ref,
    near,
    stat_cols,
    st_main,
    st_down,
    st_up,
    load_sem,
    send_sem,
    recv_sem,
    stat_send,
    stat_recv,
):
    head_count, head_size, row_count, col_count, n_tm, n_space = sizes
    tokens = row_count * col_count
    half = tokens // 2
    scale = 1.0 / math.sqrt(head_size)
    tm, sp = lax.axis_index("tm"), lax.axis_index("space")
    side = lax.rem(tm, 2)
    pair = tm + 1 - 2 * side
    other = tm - 1 + 2 * side
    relay_to = tm + 2 - 4 * side
    relay_from = tm - 2 + 4 * side
    has_other = (other >= 0) & (other < n_tm)
    has_to = (relay_to >= 0) & (relay_to < n_tm)
    has_from = (relay_from >= 0) & (relay_from < n_tm)
    has_up = sp > 0
    has_down = sp < n_space - 1

    st_main[...] = jnp.zeros_like(st_main)
    st_down[...] = jnp.zeros_like(st_down)
    st_up[...] = jnp.zeros_like(st_up)

    barrier = pltpu.get_barrier_semaphore()

    def greet(cond, tm_to, sp_to):
        @pl.when(cond)
        def _():
            pl.semaphore_signal(barrier, inc=1, device_id=(tm_to, sp_to), device_id_type=MESH)

    pl.semaphore_signal(barrier, inc=1, device_id=(pair, sp), device_id_type=MESH)
    greet(has_to, relay_to, sp)
    greet(has_from, relay_from, sp)
    greet(has_up, tm, sp - 1)
    greet(has_down, tm, sp + 1)

    near_arrays = ((k_ref, v_ref), (q_ref, g_ref))
    pieces = [(phase, h) for phase in range(2) for h in range(head_count)]
    count = len(pieces)

    def block(j, slot, start, size):
        phase, h = pieces[j]
        return near.at[phase, h, :, slot, start : start + size, :]

    def source(j, a):
        phase, h = pieces[j]
        return near_arrays[phase][a].at[:, h * head_size : (h + 1) * head_size]

    def load(j, a):
        phase, h = pieces[j]
        return pltpu.make_async_copy(
            source(j, a), near.at[phase, h, a, 0, 0:tokens, :], load_sem.at[j]
        )

    def load_wait(j):
        whole = block(j, 0, 0, tokens)
        pltpu.make_async_copy(whole, whole, load_sem.at[j]).wait()

    def remote(src, dst, send, recv, device):
        return pltpu.make_async_remote_copy(
            src_ref=src,
            dst_ref=dst,
            send_sem=send,
            recv_sem=recv,
            device_id=device,
            device_id_type=MESH,
        )

    def to_pair(j, a):
        phase, h = pieces[j]
        return remote(
            source(j, a),
            near.at[phase, h, a, 1, 0:tokens, :],
            send_sem.at[0],
            recv_sem.at[j, 0],
            (pair, sp),
        )

    def both_pair(j):
        whole = block(j, 1, 0, tokens)
        return remote(whole, whole, send_sem.at[0], recv_sem.at[j, 0], (pair, sp))

    def to_relay(j):
        return remote(
            block(j, 1, 0, tokens),
            block(j, 2, 0, tokens),
            send_sem.at[1],
            recv_sem.at[j, 1],
            (relay_to, sp),
        )

    def to_up(j, slot, size=None):
        slots = slot if size is None else slice(slot, slot + size)
        late = 1 if slot == 2 else 0
        return remote(
            block(j, slots, 0, half),
            block(j, slots, tokens, half),
            send_sem.at[2 + late],
            recv_sem.at[j, 2 + late],
            (tm, sp - 1),
        )

    def to_down(j, slot, size=None):
        slots = slot if size is None else slice(slot, slot + size)
        late = 1 if slot == 2 else 0
        return remote(
            block(j, slots, half, half),
            block(j, slots, tokens + half, half),
            send_sem.at[4 + late],
            recv_sem.at[j, 4 + late],
            (tm, sp + 1),
        )

    def rows_out(j, slot):
        @pl.when(has_up)
        def _():
            to_up(j, slot).start()

        @pl.when(has_down)
        def _():
            to_down(j, slot).start()

    def pass_on(j):
        if pieces[j][0] == 0:
            load_wait(j)
        rows_out(j, 0)
        both_pair(j).wait_recv()

        @pl.when(has_to)
        def _():
            to_relay(j).start()

        rows_out(j, 1)

    def pass_other(j):
        @pl.when(has_other)
        def _():
            to_relay(j).wait_recv()
            rows_out(j, 2)

    def arrive_halo(j):
        @pl.when(has_down)
        def _():
            to_up(j, 0, 2).wait_recv()

        @pl.when(has_up)
        def _():
            to_down(j, 0, 2).wait_recv()

        @pl.when(has_down & has_other)
        def _():
            to_up(j, 2).wait_recv()

        @pl.when(has_up & has_other)
        def _():
            to_down(j, 2).wait_recv()

    get_windows = pltpu.make_async_copy(win_hbm, win_ref, load_sem.at[count])
    get_windows.start()
    for j in range(count):
        for a in range(2):
            load(j, a).start()

    expected = (
        1
        + has_to.astype(jnp.int32)
        + has_from.astype(jnp.int32)
        + has_up.astype(jnp.int32)
        + has_down.astype(jnp.int32)
    )
    pl.semaphore_wait(barrier, expected)
    for j in range(count):
        for a in range(2):
            to_pair(j, a).start()

    @pl.when(jnp.logical_not(has_other))
    def _():
        for phase, h in pieces:
            near[phase, h, :, 2] = jnp.zeros((2, 2 * tokens, head_size), near.dtype)

    @pl.when(jnp.logical_not(has_down))
    def _():
        for phase, h in pieces:
            near[phase, h, :, :, tokens : tokens + half, :] = jnp.zeros(
                (2, 3, half, head_size), near.dtype
            )

    @pl.when(jnp.logical_not(has_up))
    def _():
        for phase, h in pieces:
            near[phase, h, :, :, tokens + half : 2 * tokens, :] = jnp.zeros(
                (2, 3, half, head_size), near.dtype
            )

    own_id = lax.broadcasted_iota(jnp.int32, (tokens, 2 * tokens), 0)
    near_id = lax.broadcasted_iota(jnp.int32, (tokens, 2 * tokens), 1)
    own_row, own_col = own_id // col_count, own_id % col_count
    near_row, near_col = near_id // col_count, near_id % col_count
    upper = near_row >= row_count + row_count // 2
    near_row = jnp.where(upper, near_row - 2 * row_count, near_row)
    global_row = sp * row_count + near_row
    row_inside = (global_row >= 0) & (global_row < n_space * row_count)
    row_gap = jnp.where(row_inside, jnp.abs(own_row - near_row), 1 << 20)
    col_gap = jnp.abs(own_col - near_col)
    other_gap = jnp.where(has_other, 0, 1 << 20)

    def window(h):
        col_in = col_gap <= win_ref[1, h]
        here = (row_gap <= win_ref[0, h]) & col_in
        there = (row_gap + other_gap <= win_ref[0, h]) & col_in
        return jnp.concatenate([here, here, there], axis=1)

    lane = lax.broadcasted_iota(jnp.int32, (tokens, tokens), 1)

    def forward(h):
        out_cols = slice(h * head_size, (h + 1) * head_size)
        query = near[1, h, 0, 0, 0:tokens, :]
        grad = near[1, h, 1, 0, 0:tokens, :]
        keys = near[0, h, 0].reshape(6 * tokens, head_size)
        vals = near[0, h, 1].reshape(6 * tokens, head_size)
        scores = jnp.where(window(h), dot_nt(query, keys) * scale, masked_score)
        top = jnp.max(scores, axis=1, keepdims=True)
        powers = jnp.exp(scores - top)
        total = jnp.sum(powers, axis=1, keepdims=True)
        soft = powers * (1.0 / total)
        attended = dot_nn(soft.astype(jnp.bfloat16), vals).astype(jnp.bfloat16)
        att_ref[:, out_cols] = attended
        out_dot = jnp.sum(
            grad.astype(jnp.float32) * attended.astype(jnp.float32), axis=1, keepdims=True
        )
        grad_scores = (soft * (dot_nt(grad, vals) - out_dot)).astype(jnp.bfloat16)
        gq_ref[:, out_cols] = (dot_nn(grad_scores, keys) * scale).astype(jnp.bfloat16)
        log_total = top + jnp.log(total)
        stats = jnp.where(lane == h, log_total, stat_cols[...])
        stat_cols[...] = jnp.where(lane == 8 + h, out_dot, stats)

    row_lane = lax.broadcasted_iota(jnp.int32, (1, tokens), 1)

    def stat_row(r):
        parts = []
        for slot in range(3):
            parts.append(st_main[slot, r : r + 1, :])
            parts.append(
                jnp.where(row_lane < half, st_down[slot, r : r + 1, :], st_up[slot, r : r + 1, :])
            )
        return jnp.concatenate(parts, axis=1)

    def backward(h):
        out_cols = slice(h * head_size, (h + 1) * head_size)
        key = near[0, h, 0, 0, 0:tokens, :]
        val = near[0, h, 1, 0, 0:tokens, :]
        queries = near[1, h, 0].reshape(6 * tokens, head_size)
        grads = near[1, h, 1].reshape(6 * tokens, head_size)
        scores = dot_nt(key, queries) * scale - stat_row(h)
        soft = jnp.exp(jnp.where(window(h), scores, masked_score))
        gv_ref[:, out_cols] = dot_nn(soft.astype(jnp.bfloat16), grads).astype(jnp.bfloat16)
        grad_scores = (soft * (dot_nt(val, grads) - stat_row(8 + h))).astype(jnp.bfloat16)
        gk_ref[:, out_cols] = (dot_nn(grad_scores, queries) * scale).astype(jnp.bfloat16)

    def stat_copies():
        targets = [
            (None, st_main.at[1], (pair, sp)),
            (has_other, st_main.at[2], (other, sp)),
        ]
        for slot, (cond, frame) in enumerate(((None, tm), (None, pair), (has_other, other))):
            for at, there, cond_s in ((st_down, sp - 1, has_up), (st_up, sp + 1, has_down)):
                both = cond_s if cond is None else cond & cond_s
                targets.append((both, at.at[slot], (frame, there)))
        arrivals = [None, has_other]
        for cond in (None, None, has_other):
            for cond_s in (has_down, has_up):
                arrivals.append(cond_s if cond is None else cond & cond_s)
        found = []
        for i, (cond, dst, device) in enumerate(targets):
            copy = pltpu.make_async_remote_copy(
                src_ref=st_main.at[0],
                dst_ref=dst,
                send_sem=stat_send.at[i],
                recv_sem=stat_recv.at[i],
                device_id=device,
                device_id_type=MESH,
            )
            found.append((cond, arrivals[i], copy))
        return found

    def when(cond, action):
        if cond is None:
            action()
        else:
            pl.when(cond)(action)

    stat_cols[...] = jnp.zeros_like(stat_cols)
    lag = 3
    slack = 2
    for h in range(head_count):
        load_wait(head_count + h)

    done = 0
    for j in range(count + lag):
        if j < count:
            pass_on(j)
        if j >= lag:
            pass_other(j - lag)
        if done < head_count and j >= min(done + lag + slack, count + lag - 1):
            last = head_count if j == count + lag - 1 else done + 1
            while done < last:
                if done == 0:
                    get_windows.wait()
                arrive_halo(done)
                forward(done)
                done += 1
            if done == head_count:
                st_main[0] = stat_cols[...].T[0:16, :]
                for cond, _, copy in stat_copies():
                    when(cond, copy.start)
    for _, cond, copy in stat_copies():
        when(cond, copy.wait_recv)
    for h in range(head_count):
        arrive_halo(head_count + h)
        backward(h)

    for cond, _, copy in stat_copies():
        when(cond, copy.wait_send)
    everything = near.at[:, :, :, 1, 0:tokens, :]
    remote(everything, everything, send_sem.at[0], recv_sem.at[0, 0], (pair, sp)).wait_send()
    when(
        has_to,
        remote(everything, everything, send_sem.at[1], recv_sem.at[0, 0], (pair, sp)).wait_send,
    )
    early = near.at[:, :, :, 0:2, 0:half, :]
    late = near.at[:, :, :, 2, 0:half, :]
    for i, cond in ((2, has_up), (4, has_down)):
        when(
            cond, remote(early, early, send_sem.at[i], recv_sem.at[0, 0], (pair, sp)).wait_send
        )
        when(
            cond & has_other,
            remote(late, late, send_sem.at[i + 1], recv_sem.at[0, 0], (pair, sp)).wait_send,
        )


def put_out(*refs):
    sources, targets, sems = refs[:4], refs[4:8], refs[8]
    copies = [pltpu.make_async_copy(sources[i], targets[i], sems.at[i]) for i in range(4)]
    for copy in copies:
        copy.start()
    for copy in copies:
        copy.wait()


def on_device(queries, key_vectors, values, grad_out, windows):
    local_shape = queries.shape
    row_count, col_count, features = local_shape[1:]
    head_count = windows.shape[1]
    head_size = features // head_count
    tokens = row_count * col_count
    sizes = (
        head_count,
        head_size,
        row_count,
        col_count,
        lax.axis_size("tm"),
        lax.axis_size("space"),
    )
    flat = (tokens, features)
    count = 2 * head_count
    outs = pl.pallas_call(
        functools.partial(kernel, sizes),
        out_shape=[jax.ShapeDtypeStruct(flat, jnp.bfloat16)] * 4,
        in_specs=[pl.BlockSpec(memory_space=pl.ANY)] * 5,
        out_specs=[pl.BlockSpec(memory_space=pltpu.VMEM)] * 4,
        scratch_shapes=[
            pltpu.SMEM((2, head_count), jnp.int32),
            pltpu.VMEM((2, head_count, 2, 3, 2 * tokens, head_size), jnp.bfloat16),
            pltpu.VMEM((tokens, tokens), jnp.float32),
            pltpu.VMEM((3, 16, tokens), jnp.float32),
            pltpu.VMEM((3, 16, tokens), jnp.float32),
            pltpu.VMEM((3, 16, tokens), jnp.float32),
            pltpu.SemaphoreType.DMA((count + 1,)),
            pltpu.SemaphoreType.DMA((6,)),
            pltpu.SemaphoreType.DMA((count, 6)),
            pltpu.SemaphoreType.DMA((8,)),
            pltpu.SemaphoreType.DMA((8,)),
        ],
        compiler_params=pltpu.CompilerParams(
            collective_id=0, has_side_effects=True, vmem_limit_bytes=55_600_000
        ),
    )(
        windows,
        queries.reshape(flat),
        key_vectors.reshape(flat),
        values.reshape(flat),
        grad_out.reshape(flat),
    )
    outs = pl.pallas_call(
        put_out,
        out_shape=[jax.ShapeDtypeStruct(flat, jnp.bfloat16)] * 4,
        in_specs=[pl.BlockSpec(memory_space=pltpu.VMEM)] * 4,
        out_specs=[pl.BlockSpec(memory_space=pltpu.HBM)] * 4,
        scratch_shapes=[
            pltpu.SemaphoreType.DMA((4,)),
        ],
        compiler_params=pltpu.CompilerParams(vmem_limit_bytes=4_000_000),
    )(*outs)
    return tuple(out.reshape(local_shape) for out in outs)


def solution(mesh):
    spec = P("tm", "space", None, None)
    return jax.shard_map(
        on_device,
        mesh=mesh,
        in_specs=(spec, spec, spec, spec, P()),
        out_specs=(spec, spec, spec, spec),
        check_vma=False,
    )
```

profile of v0, /device:TPU:0, one launch (start us, length us, event | category | flops | bytes accessed | tf_op | source)
XLA Modules:
  0.0 31.8 jit_solution(4713910599167528217)
XLA Ops:
  0.6 0.0 copy-start
  0.6 0.7 %copy-done = s32[2,6]{1,0:T(2,128)S(1)} copy-done((s32[2,6]{1,0:T(2,128)S(1)}, s32[2,6]{1,0:T(2,128)}, u32[]{:S(2)}) %copy-start) | copy-done | bytes 72
  1.3 29.6 %shard_map.84 = (bf16[128,768]{1,0:T(8,128)(2,1)S(1)}, bf16[128,768]{1,0:T(8,128)(2,1)S(1)}, bf16[128,768]{1,0:T(8,128)(2,1)S(1)}, bf16[128,768]{1,0:T(8,128)(2,1)S(1)}) custom-call(s32[2,6]{1,0:T(2,128)S(1)} %copy-done, bf16[128,768]{1,0:T(8,128)(2,1)} %bitcast.8, bf16[128,768]{1,0:T(8,128)(2,1)} %bitcast.9, bf16[128,768]{1,0:T(8,128)(2,1)} %bitcast.10, ...), custom_call_target="tpu_custom_call" | custom-call | tf_op jit(solution)/shard_map/pallas_call | solution.py:409
  30.9 0.9 %shard_map.85 = (bf16[128,768]{1,0:T(8,128)(2,1)}, bf16[128,768]{1,0:T(8,128)(2,1)}, bf16[128,768]{1,0:T(8,128)(2,1)}, bf16[128,768]{1,0:T(8,128)(2,1)}) custom-call(bf16[128,768]{1,0:T(8,128)(2,1)S(1)} %get-tuple-element.12.refs_0_, bf16[128,768]{1,0:T(8,128)(2,1)S(1)} %get-tuple-element.13.refs_1_, bf16[128,768]{1,0:T(8,128)(2,1)S(1)} %get-tuple-element.14.refs_2_, ...), custom_call_target="tpu_custom_call" | custom-call | tf_op jit(solution)/shard_map/pallas_call | solution.py:437
Async XLA Ops:
  0.6 0.7 %copy-start = (s32[2,6]{1,0:T(2,128)S(1)}, s32[2,6]{1,0:T(2,128)}, u32[]{:S(2)}) copy-start(s32[2,6]{1,0:T(2,128)} %win_hbm.1) | copy-start | bytes 148
where the time goes:
time: 32.4 us; the launch traced here: 31.8 us
  Pallas kernels  30.5 us (94%)
  local copies, waits for them, and re-layouts  0.67 us (2%)
  between operations  0.65 us (2%)
    pallas_call x1, Pallas kernels, on_device(): pl.pallas_call(functools.partial(kernel, sizes), out_shape=[jax.ShapeDtyp...  29.6 us
    pallas_call x1, Pallas kernels, on_device(): pl.pallas_call(put_out, out_shape=[jax.ShapeDtypeStruct(flat, jnp.bfloat1...  0.91 us
    unnamed x2, local copies, waits for them, and re-layouts  0.67 us

commit v1 on v0

v1 whole, which is shorter than its diff:
```python
import functools
import math

import jax
import jax.numpy as jnp
from jax import lax
from jax.experimental import pallas as pl
from jax.experimental.pallas import tpu as pltpu
from jax.sharding import PartitionSpec as P

masked_score = -1e30
MESH = pl.DeviceIdType.MESH

STEPS = {"A": 0.0, "B": 1.05, "C": 1.9, "D": 3.4, "E": 5.0, "F": 6.6}

IN_PAIR, IN_OTHER, HALO_UP, HALO_DOWN, BACK_UP, BACK_DOWN, BACK_OTHER, BACK_PAIR = (
    0,
    1,
    2,
    5,
    8,
    11,
    14,
    15,
)
KINDS = 16


def dot_nt(a, b):
    return lax.dot_general(a, b, (((1,), (1,)), ((), ())), preferred_element_type=jnp.float32)


def dot_nn(a, b):
    return lax.dot_general(a, b, (((1,), (0,)), ((), ())), preferred_element_type=jnp.float32)


def dot_tn(a, b):
    return lax.dot_general(a, b, (((0,), (0,)), ((), ())), preferred_element_type=jnp.float32)


def kernel(
    sizes,
    win_hbm,
    q_ref,
    k_ref,
    v_ref,
    g_ref,
    att_ref,
    gq_ref,
    gk_ref,
    gv_ref,
    win_ref,
    near,
    own,
    part,
    back_out,
    back_in,
    other_out,
    other_in,
    pair_out,
    pair_in,
    row_gap,
    col_gap,
    load_sem,
    send_sem,
    recv_sem,
):
    head_count, head_size, row_count, col_count, n_tm, n_space = sizes
    tokens = row_count * col_count
    half = tokens // 2
    scale = 1.0 / math.sqrt(head_size)
    tm, sp = lax.axis_index("tm"), lax.axis_index("space")
    side = lax.rem(tm, 2)
    pair = tm + 1 - 2 * side
    relay_to = tm + 2 - 4 * side
    relay_from = tm - 2 + 4 * side
    has_to = (relay_to >= 0) & (relay_to < n_tm)
    has_other = (relay_from >= 0) & (relay_from < n_tm)
    has_up = sp > 0
    has_down = sp < n_space - 1
    heads = range(head_count)

    def when(cond, action):
        if cond is None:
            action()
        else:
            pl.when(cond)(action)

    def load(h, a):
        ref = (k_ref, v_ref, q_ref, g_ref)[a]
        target = near.at[h, a, 0, 0:tokens, :] if a < 2 else own.at[h, a - 2]
        return pltpu.make_async_copy(
            ref.at[:, h * head_size : (h + 1) * head_size],
            target,
            load_sem.at[h, a // 2],
        )

    def load_wait(h, first):
        whole = near.at[h, :, 0, 0:tokens, :] if first else own.at[h]
        pltpu.make_async_copy(whole, whole, load_sem.at[h, 0 if first else 1]).wait()

    barrier = pltpu.get_barrier_semaphore()

    def greet(cond, tm_to, sp_to):
        def signal():
            pl.semaphore_signal(barrier, inc=1, device_id=(tm_to, sp_to), device_id_type=MESH)

        when(cond, signal)

    greet(None, pair, sp)
    greet(has_to, relay_to, sp)
    greet(has_other, relay_from, sp)
    greet(has_up, tm, sp - 1)
    greet(has_down, tm, sp + 1)
    get_windows = pltpu.make_async_copy(win_hbm, win_ref, load_sem.at[head_count, 0])
    for h in heads:
        for a in range(2):
            load(h, a).start()
    get_windows.start()
    for h in heads:
        for a in range(2, 4):
            load(h, a).start()

    def remote(src, dst, send, recv, device):
        return pltpu.make_async_remote_copy(
            src_ref=src,
            dst_ref=dst,
            send_sem=send,
            recv_sem=recv,
            device_id=device,
            device_id_type=MESH,
        )

    def to_pair(h):
        return remote(
            near.at[h, :, 0, 0:tokens, :],
            near.at[h, :, 1, 0:tokens, :],
            send_sem.at[0],
            recv_sem.at[h, IN_PAIR],
            (pair, sp),
        )

    def to_relay(h):
        return remote(
            near.at[h, :, 1, 0:tokens, :],
            near.at[h, :, 2, 0:tokens, :],
            send_sem.at[1],
            recv_sem.at[h, IN_OTHER],
            (relay_to, sp),
        )

    def halo_up(h, slot):
        return remote(
            near.at[h, :, slot, 0:half, :],
            near.at[h, :, slot, tokens : tokens + half, :],
            send_sem.at[2 + slot // 2],
            recv_sem.at[h, HALO_UP + slot],
            (tm, sp - 1),
        )

    def halo_down(h, slot):
        return remote(
            near.at[h, :, slot, half:tokens, :],
            near.at[h, :, slot, tokens + half : 2 * tokens, :],
            send_sem.at[4 + slot // 2],
            recv_sem.at[h, HALO_DOWN + slot],
            (tm, sp + 1),
        )

    def back_up(h, slot):
        return remote(
            back_out.at[h, slot, 1],
            back_in.at[h, slot, 1],
            send_sem.at[6 + slot // 2],
            recv_sem.at[h, BACK_UP + slot],
            (tm, sp - 1),
        )

    def back_down(h, slot):
        return remote(
            back_out.at[h, slot, 0],
            back_in.at[h, slot, 0],
            send_sem.at[8 + slot // 2],
            recv_sem.at[h, BACK_DOWN + slot],
            (tm, sp + 1),
        )

    def back_other(h):
        return remote(
            other_out.at[h],
            other_in.at[h],
            send_sem.at[10],
            recv_sem.at[h, BACK_OTHER],
            (relay_from, sp),
        )

    def back_pair(h):
        return remote(
            pair_out.at[h],
            pair_in.at[h],
            send_sem.at[11],
            recv_sem.at[h, BACK_PAIR],
            (pair, sp),
        )

    def halos(h, slot):
        when(has_up, lambda: halo_up(h, slot).start())
        when(has_down, lambda: halo_down(h, slot).start())

    expected = (
        1
        + has_to.astype(jnp.int32)
        + has_other.astype(jnp.int32)
        + has_up.astype(jnp.int32)
        + has_down.astype(jnp.int32)
    )
    pl.semaphore_wait(barrier, expected)
    for h in heads:
        load_wait(h, True)
        to_pair(h).start()
    for h in heads:
        halos(h, 0)

    @pl.when(jnp.logical_not(has_other))
    def _():
        near[:, :, 2] = jnp.zeros((head_count, 2, 2 * tokens, head_size), near.dtype)

    @pl.when(jnp.logical_not(has_to))
    def _():
        other_in[...] = jnp.zeros_like(other_in)

    @pl.when(jnp.logical_not(has_down))
    def _():
        near[:, :, :, tokens : tokens + half, :] = jnp.zeros(
            (head_count, 2, 3, half, head_size), near.dtype
        )
        back_in[:, :, 1] = jnp.zeros((head_count, 3, 2, half, head_size), near.dtype)

    @pl.when(jnp.logical_not(has_up))
    def _():
        near[:, :, :, tokens + half :, :] = jnp.zeros(
            (head_count, 2, 3, half, head_size), near.dtype
        )
        back_in[:, :, 0] = jnp.zeros((head_count, 3, 2, half, head_size), near.dtype)

    near_id = lax.broadcasted_iota(jnp.int32, (2 * tokens, tokens), 0)
    own_id = lax.broadcasted_iota(jnp.int32, (2 * tokens, tokens), 1)
    own_row, own_col = own_id // col_count, own_id % col_count
    near_row, near_col = near_id // col_count, near_id % col_count
    upper = near_row >= row_count + row_count // 2
    near_row = jnp.where(upper, near_row - 2 * row_count, near_row)
    global_row = sp * row_count + near_row
    row_inside = (global_row >= 0) & (global_row < n_space * row_count)
    row_gap[...] = jnp.where(row_inside, jnp.abs(own_row - near_row), 1 << 20)
    col_gap[...] = jnp.abs(own_col - near_col)

    for h in heads:
        load_wait(h, False)
    get_windows.wait()

    def compute(h):
        cols = slice(h * head_size, (h + 1) * head_size)
        query, grad = own[h, 0], own[h, 1]
        keys = near[h, 0].reshape(6 * tokens, head_size)
        vals = near[h, 1].reshape(6 * tokens, head_size)
        row_reach, col_reach = win_ref[0, h], win_ref[1, h]
        col_in = col_gap[...] <= col_reach
        here = (row_gap[...] <= row_reach) & col_in
        there = (row_gap[...] <= jnp.where(has_other, row_reach, -1)) & col_in
        window = jnp.concatenate([here, here, there], axis=0)
        scores = jnp.where(window, dot_nt(keys, query) * scale, masked_score)
        top = jnp.max(scores, axis=0, keepdims=True)
        powers = jnp.exp(scores - top)
        total = jnp.sum(powers, axis=0, keepdims=True)
        soft = powers * (1.0 / total)
        weights = soft.astype(jnp.bfloat16)
        grad_weights = dot_nt(vals, grad)
        out_dot = jnp.sum(soft * grad_weights, axis=0, keepdims=True)
        grad_scores = (soft * (grad_weights - out_dot)).astype(jnp.bfloat16)
        for a, partial in ((0, dot_nn(grad_scores, query)), (1, dot_nn(weights, grad))):
            for slot in range(3):
                at = 2 * slot * tokens
                part[h, slot, a] = partial[at : at + tokens]
                back_out[h, slot, 0, a] = partial[at + tokens : at + tokens + half].astype(
                    jnp.bfloat16
                )
                back_out[h, slot, 1, a] = partial[at + tokens + half : at + 2 * tokens].astype(
                    jnp.bfloat16
                )
        for slot in (2, 1, 0):
            cond_up = has_up if slot < 2 else has_up & has_other
            cond_down = has_down if slot < 2 else has_down & has_other
            when(cond_up, lambda: back_up(h, slot).start())
            when(cond_down, lambda: back_down(h, slot).start())
        att_ref[:, cols] = dot_tn(weights, vals).astype(jnp.bfloat16)
        gq_ref[:, cols] = (dot_tn(grad_scores, keys) * scale).astype(jnp.bfloat16)

    def step_a(h):
        to_pair(h).wait_recv()
        when(has_to, lambda: to_relay(h).start())
        halos(h, 1)

    def step_b(h):
        @pl.when(has_other)
        def _():
            to_relay(h).wait_recv()
            halos(h, 2)

    def step_c(h):
        @pl.when(has_down)
        def _():
            halo_up(h, 0).wait_recv()
            halo_up(h, 1).wait_recv()

        @pl.when(has_up)
        def _():
            halo_down(h, 0).wait_recv()
            halo_down(h, 1).wait_recv()

        when(has_down & has_other, lambda: halo_up(h, 2).wait_recv())
        when(has_up & has_other, lambda: halo_down(h, 2).wait_recv())
        compute(h)

    def arrive_back(h, slot):
        when(has_down, lambda: back_up(h, slot).wait_recv())
        when(has_up, lambda: back_down(h, slot).wait_recv())

    def summed(h, slot, a):
        halo = jnp.concatenate([back_in[h, slot, 0, a], back_in[h, slot, 1, a]], axis=0)
        return part[h, slot, a] + halo.astype(jnp.float32)

    def step_d(h):
        @pl.when(has_other)
        def _():
            arrive_back(h, 2)
            for a in range(2):
                other_out[h, a] = summed(h, 2, a).astype(jnp.bfloat16)
            back_other(h).start()

    def step_e(h):
        arrive_back(h, 1)
        when(has_to, lambda: back_other(h).wait_recv())
        for a in range(2):
            pair_out[h, a] = (summed(h, 1, a) + other_in[h, a].astype(jnp.float32)).astype(
                jnp.bfloat16
            )
        back_pair(h).start()

    def step_f(h):
        cols = slice(h * head_size, (h + 1) * head_size)
        arrive_back(h, 0)
        back_pair(h).wait_recv()
        key_sum = summed(h, 0, 0) + pair_in[h, 0].astype(jnp.float32)
        gk_ref[:, cols] = (key_sum * scale).astype(jnp.bfloat16)
        value_sum = summed(h, 0, 1) + pair_in[h, 1].astype(jnp.float32)
        gv_ref[:, cols] = value_sum.astype(jnp.bfloat16)

    steps = {"A": step_a, "B": step_b, "C": step_c, "D": step_d, "E": step_e, "F": step_f}
    order = sorted((h + STEPS[name], name, h) for name in steps for h in heads)
    for _, name, h in order:
        steps[name](h)

    def drain(cond, ref, i):
        when(cond, remote(ref, ref, send_sem.at[i], recv_sem.at[0, 0], (pair, sp)).wait_send)

    mine = near.at[:, :, 1, 0:tokens, :]
    early = near.at[:, :, 0:2, 0:half, :]
    late = near.at[:, :, 2, 0:half, :]
    drain(None, mine, 0)
    drain(has_to, mine, 1)
    for i, cond in ((2, has_up), (4, has_down), (6, has_up), (8, has_down)):
        drain(cond, early, i)
        drain(cond & has_other, late, i + 1) if i < 6 else None
    drain(has_up & has_other, late, 7)
    drain(has_down & has_other, late, 9)
    drain(has_other, other_out, 10)
    drain(None, pair_out, 11)


def put_out(*refs):
    sources, targets, sems = refs[:4], refs[4:8], refs[8]
    copies = [pltpu.make_async_copy(sources[i], targets[i], sems.at[i]) for i in range(4)]
    for copy in copies:
        copy.start()
    for copy in copies:
        copy.wait()


def on_device(queries, key_vectors, values, grad_out, windows):
    local_shape = queries.shape
    row_count, col_count, features = local_shape[1:]
    head_count = windows.shape[1]
    head_size = features // head_count
    tokens = row_count * col_count
    half = tokens // 2
    sizes = (
        head_count,
        head_size,
        row_count,
        col_count,
        lax.axis_size("tm"),
        lax.axis_size("space"),
    )
    flat = (tokens, features)
    low = jnp.bfloat16
    outs = pl.pallas_call(
        functools.partial(kernel, sizes),
        out_shape=[jax.ShapeDtypeStruct(flat, low)] * 4,
        in_specs=[pl.BlockSpec(memory_space=pltpu.HBM)] * 5,
        out_specs=[pl.BlockSpec(memory_space=pltpu.VMEM)] * 4,
        scratch_shapes=[
            pltpu.SMEM((2, head_count), jnp.int32),
            pltpu.VMEM((head_count, 2, 3, 2 * tokens, head_size), low),
            pltpu.VMEM((head_count, 2, tokens, head_size), low),
            pltpu.VMEM((head_count, 3, 2, tokens, head_size), jnp.float32),
            pltpu.VMEM((head_count, 3, 2, 2, half, head_size), low),
            pltpu.VMEM((head_count, 3, 2, 2, half, head_size), low),
            pltpu.VMEM((head_count, 2, tokens, head_size), low),
            pltpu.VMEM((head_count, 2, tokens, head_size), low),
            pltpu.VMEM((head_count, 2, tokens, head_size), low),
            pltpu.VMEM((head_count, 2, tokens, head_size), low),
            pltpu.VMEM((2 * tokens, tokens), jnp.int32),
            pltpu.VMEM((2 * tokens, tokens), jnp.int32),
            pltpu.SemaphoreType.DMA((head_count + 1, 2)),
            pltpu.SemaphoreType.DMA((12,)),
            pltpu.SemaphoreType.DMA((head_count, KINDS)),
        ],
        compiler_params=pltpu.CompilerParams(
            collective_id=0, has_side_effects=True, vmem_limit_bytes=55_600_000
        ),
    )(
        windows,
        queries.reshape(flat),
        key_vectors.reshape(flat),
        values.reshape(flat),
        grad_out.reshape(flat),
    )
    outs = pl.pallas_call(
        put_out,
        out_shape=[jax.ShapeDtypeStruct(flat, low)] * 4,
        in_specs=[pl.BlockSpec(memory_space=pltpu.VMEM)] * 4,
        out_specs=[pl.BlockSpec(memory_space=pltpu.HBM)] * 4,
        scratch_shapes=[
            pltpu.SemaphoreType.DMA((4,)),
        ],
        compiler_params=pltpu.CompilerParams(vmem_limit_bytes=4_000_000),
    )(*outs)
    return tuple(out.reshape(local_shape) for out in outs)


def solution(mesh):
    spec = P("tm", "space", None, None)
    return jax.shard_map(
        on_device,
        mesh=mesh,
        in_specs=(spec, spec, spec, spec, P()),
        out_specs=(spec, spec, spec, spec),
        check_vma=False,
    )
```

time: 32.4 us -> 48.1 us (1.48)
  the two profiles are of different devices: /device:TPU:0 before, /device:TPU:1 now
where the time goes in v1:
time: 48.1 us; the launch traced here: 47.9 us
  Pallas kernels  46.6 us (97%)
  local copies, waits for them, and re-layouts  0.67 us (1%)
  between operations  0.65 us (1%)
    pallas_call x1, Pallas kernels, on_device(): pl.pallas_call(functools.partial(kernel, sizes), out_shape=[jax.ShapeDtyp...  45.7 us

profile of v1, /device:TPU:1, one launch (start us, length us, event | category | flops | bytes accessed | tf_op | source)
XLA Modules:
  0.0 47.9 jit_solution(9388921006061400757)
XLA Ops:
  0.6 0.0 copy-start
  0.6 0.7 %copy-done = s32[2,6]{1,0:T(2,128)S(1)} copy-done((s32[2,6]{1,0:T(2,128)S(1)}, s32[2,6]{1,0:T(2,128)}, u32[]{:S(2)}) %copy-start) | copy-done | bytes 72
  1.3 45.7 %shard_map.84 = (bf16[128,768]{1,0:T(8,128)(2,1)S(1)}, bf16[128,768]{1,0:T(8,128)(2,1)S(1)}, bf16[128,768]{1,0:T(8,128)(2,1)S(1)}, bf16[128,768]{1,0:T(8,128)(2,1)S(1)}) custom-call(s32[2,6]{1,0:T(2,128)S(1)} %copy-done, bf16[128,768]{1,0:T(8,128)(2,1)} %bitcast.8, bf16[128,768]{1,0:T(8,128)(2,1)} %bitcast.9, bf16[128,768]{1,0:T(8,128)(2,1)} %bitcast.10, ...), custom_call_target="tpu_custom_call" | custom-call | tf_op jit(solution)/shard_map/pallas_call | solution.py:406
  47.0 0.9 %shard_map.85 = (bf16[128,768]{1,0:T(8,128)(2,1)}, bf16[128,768]{1,0:T(8,128)(2,1)}, bf16[128,768]{1,0:T(8,128)(2,1)}, bf16[128,768]{1,0:T(8,128)(2,1)}) custom-call(bf16[128,768]{1,0:T(8,128)(2,1)S(1)} %get-tuple-element.12.refs_0_, bf16[128,768]{1,0:T(8,128)(2,1)S(1)} %get-tuple-element.13.refs_1_, bf16[128,768]{1,0:T(8,128)(2,1)S(1)} %get-tuple-element.14.refs_2_, ...), custom_call_target="tpu_custom_call" | custom-call | tf_op jit(solution)/shard_map/pallas_call | solution.py:438
Async XLA Ops:
  0.6 0.7 %copy-start = (s32[2,6]{1,0:T(2,128)S(1)}, s32[2,6]{1,0:T(2,128)}, u32[]{:S(2)}) copy-start(s32[2,6]{1,0:T(2,128)} %win_hbm.1) | copy-start | bytes 148

commit v2 on v0

v2 whole, which is shorter than its diff:
```python
import functools
import math

import jax
import jax.numpy as jnp
from jax import lax
from jax.experimental import pallas as pl
from jax.experimental.pallas import tpu as pltpu
from jax.sharding import PartitionSpec as P

masked_score = -1e30
MESH = pl.DeviceIdType.MESH

OUTER, OWN, PAIR, FAR = range(4)

FROM_PAIR, TO_FAR, TO_OUTER = range(3)


def dot_nt(a, b):
    return lax.dot_general(a, b, (((1,), (1,)), ((), ())), preferred_element_type=jnp.float32)


def dot_nn(a, b):
    return lax.dot_general(a, b, (((1,), (0,)), ((), ())), preferred_element_type=jnp.float32)


def when(cond, action):
    if cond is None:
        action()
    else:
        pl.when(cond)(action)


def both(a, b):
    if a is None:
        return b
    return a if b is None else a & b


def kernel(
    sizes,
    win_hbm,
    q_ref,
    k_ref,
    v_ref,
    g_ref,
    att_ref,
    gq_ref,
    gk_ref,
    gv_ref,
    win_ref,
    bias,
    staged,
    near,
    results,
    st_main,
    st_down,
    st_up,
    load_sem,
    win_sem,
    send_sem,
    piece_sem,
    halo_sem,
    result_sem,
    stat_send,
    stat_recv,
):
    head_count, head_size, row_count, col_count, n_tm, n_space = sizes
    tokens = row_count * col_count
    half = tokens // 2
    mine = head_count // 2
    scale = 1.0 / math.sqrt(head_size)
    scale2 = scale * math.log2(math.e)
    tm, sp = lax.axis_index("tm"), lax.axis_index("space")
    side = lax.rem(tm, 2)
    pair = tm + 1 - 2 * side
    inner_to = tm + 2 - 4 * side
    outer_to = tm - 2 + 4 * side
    has_far = (inner_to >= 0) & (inner_to < n_tm)
    has_outer = (outer_to >= 0) & (outer_to < n_tm)
    has_up = sp > 0
    has_down = sp < n_space - 1
    held = {OUTER: has_outer, OWN: None, PAIR: None, FAR: has_far}
    heads = range(mine)
    pieces = [(phase, j, a) for phase in range(2) for j in heads for a in range(2)]
    ins = ((k_ref, v_ref), (q_ref, g_ref))
    outs = (att_ref, gq_ref, gk_ref, gv_ref)

    def head_cols(j, of_pair=False):
        first = (1 - side if of_pair else side) * mine + j
        return pl.ds(pl.multiple_of(first * head_size, head_size), head_size)

    st_main[...] = jnp.zeros_like(st_main)
    st_down[...] = jnp.zeros_like(st_down)
    st_up[...] = jnp.zeros_like(st_up)

    barrier = pltpu.get_barrier_semaphore()

    def greet(cond, tm_to, sp_to):
        def signal():
            pl.semaphore_signal(barrier, inc=1, device_id=(tm_to, sp_to), device_id_type=MESH)

        when(cond, signal)

    greet(None, pair, sp)
    greet(has_far, inner_to, sp)
    greet(has_outer, outer_to, sp)
    greet(has_up, tm, sp - 1)
    greet(has_down, tm, sp + 1)

    def main_rows(i, slot):
        phase, j, a = pieces[i]
        return near.at[phase, j, a, slot, 0:tokens, :]

    def load(i, of_pair):
        phase, j, a = pieces[i]
        return pltpu.make_async_copy(
            ins[phase][a].at[:, head_cols(j, of_pair)],
            staged.at[i] if of_pair else main_rows(i, OWN),
            load_sem.at[i, 1 if of_pair else 0],
        )

    for of_pair in (True, False):
        for i in range(len(pieces)):
            load(i, of_pair).start()
    get_windows = pltpu.make_async_copy(win_hbm, win_ref, win_sem)
    get_windows.start()

    def remote(src, dst, send, recv, device):
        return pltpu.make_async_remote_copy(
            src_ref=src,
            dst_ref=dst,
            send_sem=send,
            recv_sem=recv,
            device_id=device,
            device_id_type=MESH,
        )

    def to_pair(i):
        return remote(
            staged.at[i],
            main_rows(i, PAIR),
            send_sem.at[0],
            piece_sem.at[i, FROM_PAIR],
            (pair, sp),
        )

    def own_to_far(i):
        return remote(
            main_rows(i, OWN),
            main_rows(i, FAR),
            send_sem.at[1],
            piece_sem.at[i, TO_FAR],
            (outer_to, sp),
        )

    def pair_to_outer(i):
        return remote(
            main_rows(i, PAIR),
            main_rows(i, OUTER),
            send_sem.at[2],
            piece_sem.at[i, TO_OUTER],
            (inner_to, sp),
        )

    def halo_up(i, slot):
        phase, j, a = pieces[i]
        rows = near.at[phase, j, a, slot]
        return remote(
            rows.at[0:half, :],
            rows.at[tokens : tokens + half, :],
            send_sem.at[3 + slot],
            halo_sem.at[phase * mine + j, slot, 0],
            (tm, sp - 1),
        )

    def halo_down(i, slot):
        phase, j, a = pieces[i]
        rows = near.at[phase, j, a, slot]
        return remote(
            rows.at[half:tokens, :],
            rows.at[tokens + half : 2 * tokens, :],
            send_sem.at[7 + slot],
            halo_sem.at[phase * mine + j, slot, 1],
            (tm, sp + 1),
        )

    def halos(i, slot):
        when(has_up, lambda: halo_up(i, slot).start())
        when(has_down, lambda: halo_down(i, slot).start())

    expected = (
        1
        + has_far.astype(jnp.int32)
        + has_outer.astype(jnp.int32)
        + has_up.astype(jnp.int32)
        + has_down.astype(jnp.int32)
    )
    pl.semaphore_wait(barrier, expected)
    for i in range(len(pieces)):
        load(i, True).wait()
        to_pair(i).start()
    for i in range(len(pieces)):
        load(i, False).wait()
        when(has_outer, lambda: own_to_far(i).start())
        halos(i, OWN)

    def clear(slots, rows):
        count = rows.stop - rows.start
        for phase in range(2):
            for j in heads:
                for slot in slots:
                    near[phase, j, :, slot, rows, :] = jnp.zeros(
                        (2, count, head_size), near.dtype
                    )

    slots = (OUTER, OWN, PAIR, FAR)
    pl.when(jnp.logical_not(has_outer))(lambda: clear((OUTER,), slice(0, 2 * tokens)))
    pl.when(jnp.logical_not(has_far))(lambda: clear((FAR,), slice(0, 2 * tokens)))
    pl.when(jnp.logical_not(has_down))(lambda: clear(slots, slice(tokens, tokens + half)))
    pl.when(jnp.logical_not(has_up))(lambda: clear(slots, slice(tokens + half, 2 * tokens)))

    own_id = lax.broadcasted_iota(jnp.int32, (tokens, 2 * tokens), 0)
    near_id = lax.broadcasted_iota(jnp.int32, (tokens, 2 * tokens), 1)
    own_row, own_col = own_id // col_count, own_id % col_count
    near_row, near_col = near_id // col_count, near_id % col_count
    upper = near_row >= row_count + row_count // 2
    near_row = jnp.where(upper, near_row - 2 * row_count, near_row)
    global_row = sp * row_count + near_row
    row_inside = (global_row >= 0) & (global_row < n_space * row_count)
    row_gap = jnp.where(row_inside, jnp.abs(own_row - near_row), 1 << 20)
    col_gap = jnp.abs(own_col - near_col)

    get_windows.wait()
    for j in heads:
        h = side * mine + j
        inside = (row_gap <= win_ref[0, h]) & (col_gap <= win_ref[1, h])
        bias[j] = jnp.where(inside, 0.0, masked_score)

    def window(j, frame):
        here = bias[j]
        there = here + jnp.where(has_outer if frame == OWN else has_far, 0.0, masked_score)
        order = [there, here, here] if frame == OWN else [here, here, there]
        return jnp.concatenate(order, axis=1)

    def around(phase, j, a, frame):
        return near[phase, j, a, frame - 1 : frame + 2].reshape(6 * tokens, head_size)

    def put(kind, j, frame, value):
        if frame == OWN:
            outs[kind][:, head_cols(j)] = value
        else:
            results[kind, j] = value

    def give(kind, j):
        return remote(
            results.at[kind, j],
            outs[kind].at[:, head_cols(j)],
            send_sem.at[11],
            result_sem.at[kind, j],
            (pair, sp),
        )

    def forward(j, frame):
        query = near[1, j, 0, frame, 0:tokens, :]
        grad = near[1, j, 1, frame, 0:tokens, :]
        keys, vals = around(0, j, 0, frame), around(0, j, 1, frame)
        scores = dot_nt(query, keys) * scale2 + window(j, frame)
        top = jnp.max(scores, axis=1, keepdims=True)
        powers = jnp.exp2(scores - top)
        total = jnp.sum(powers, axis=1, keepdims=True)
        share = 1.0 / total
        attended = dot_nn(powers.astype(jnp.bfloat16), vals) * share
        put(0, j, frame, attended.astype(jnp.bfloat16))
        grad_weights = dot_nt(grad, vals)
        out_dot = jnp.sum(powers * grad_weights, axis=1, keepdims=True) * share
        grad_scores = (powers * (grad_weights - out_dot)).astype(jnp.bfloat16)
        put(1, j, frame, (dot_nn(grad_scores, keys) * (share * scale)).astype(jnp.bfloat16))
        return top + jnp.log2(total), out_dot

    row_lane = lax.broadcasted_iota(jnp.int32, (1, tokens), 1)

    def stat_row(j, r, frame):
        parts = []
        for slot in range(frame - 1, frame + 2):
            parts.append(st_main[j, slot, r : r + 1, :])
            down, up = st_down[j, slot, r : r + 1, :], st_up[j, slot, r : r + 1, :]
            parts.append(jnp.where(row_lane < half, down, up))
        return jnp.concatenate(parts, axis=1)

    def backward(j, frame):
        key = near[0, j, 0, frame, 0:tokens, :]
        val = near[0, j, 1, frame, 0:tokens, :]
        queries, grads = around(1, j, 0, frame), around(1, j, 1, frame)
        scores = dot_nt(key, queries) * scale2 + window(j, frame)
        soft = jnp.exp2(scores - stat_row(j, 0, frame))
        put(3, j, frame, dot_nn(soft.astype(jnp.bfloat16), grads).astype(jnp.bfloat16))
        grad_scores = soft * (dot_nt(val, grads) - stat_row(j, 1, frame))
        key_sum = dot_nn(grad_scores.astype(jnp.bfloat16), queries)
        put(2, j, frame, (key_sum * scale).astype(jnp.bfloat16))

    def stat_copies(j):
        far_frame, near_frame = st_main.at[j, PAIR], st_main.at[j, OWN]
        both_frames = slice(OWN, PAIR + 1)
        found = [
            (has_far, far_frame, st_main.at[j, OUTER], (inner_to, sp), has_outer),
            (has_outer, near_frame, st_main.at[j, FAR], (outer_to, sp), has_far),
        ]
        for at, there, goes, comes in (
            (st_down, sp - 1, has_up, has_down),
            (st_up, sp + 1, has_down, has_up),
        ):
            found += [
                (goes, st_main.at[j, both_frames], at.at[j, both_frames], (tm, there), comes),
                (goes & has_far, far_frame, at.at[j, OUTER], (inner_to, there), comes & has_outer),
                (goes & has_outer, near_frame, at.at[j, FAR], (outer_to, there), comes & has_far),
            ]
        return [
            (goes, comes, remote(src, dst, stat_send.at[j, i], stat_recv.at[j, i], device))
            for i, (goes, src, dst, device, comes) in enumerate(found)
        ]

    def step_pair_in(i):
        to_pair(i).wait_recv()
        when(has_far, lambda: pair_to_outer(i).start())
        halos(i, PAIR)

    def step_far_in(i):
        @pl.when(has_far)
        def _():
            own_to_far(i).wait_recv()
            halos(i, FAR)

    def step_outer_in(i):
        @pl.when(has_outer)
        def _():
            pair_to_outer(i).wait_recv()
            halos(i, OUTER)

    def arrive_halos(phase, j, slots):
        for slot in slots:
            rows = near.at[phase, j, :, slot, 0:half, :]
            for side_in, cond in ((0, has_down), (1, has_up)):
                sem = halo_sem.at[phase * mine + j, slot, side_in]
                copy = remote(rows, rows, send_sem.at[0], sem, (pair, sp))
                when(both(cond, held[slot]), copy.wait_recv)

    stats = {}

    def step_forward_pair(j):
        arrive_halos(0, j, (OWN, PAIR, FAR))
        stats[j] = forward(j, PAIR)
        for kind in (0, 1):
            give(kind, j).start()

    def step_forward_own(j):
        arrive_halos(0, j, (OUTER,))
        found = (*forward(j, OWN), *stats.pop(j))
        lane = lax.broadcasted_iota(jnp.int32, (tokens, tokens), 1)
        spread = jnp.zeros((tokens, tokens), jnp.float32)
        for at, column in zip((0, 1, 8, 9), found, strict=True):
            spread = jnp.where(lane == at, column, spread)
        st_main[j, OWN : PAIR + 1] = spread.T[0:16, :].reshape(2, 8, tokens)
        for goes, _, copy in stat_copies(j):
            when(goes, copy.start)

    def step_backward_pair(j):
        arrive_halos(1, j, (OWN, PAIR, FAR, OUTER))
        for _, comes, copy in stat_copies(j):
            when(comes, copy.wait_recv)
        backward(j, PAIR)
        for kind in (2, 3):
            give(kind, j).start()

    def step_backward_own(j):
        backward(j, OWN)

    times = []
    for i in range(len(pieces)):
        times.append((4.6 + 0.7 * i, step_pair_in, i))
        times.append((4.65 + 0.7 * i, step_far_in, i))
        times.append((7.0 + 0.7 * i, step_outer_in, i))
    for j in heads:
        times.append((9.7 + 1.4 * j, step_forward_pair, j))
        times.append((10.3 + 1.4 * j, step_forward_own, j))
        times.append((13.9 + 1.4 * j, step_backward_pair, j))
        times.append((14.5 + 1.4 * j, step_backward_own, j))
    for _, step, index in sorted(times, key=lambda entry: entry[0]):
        step(index)

    for kind in range(4):
        for j in heads:
            give(kind, j).wait_recv()

    def drain(cond, ref, i):
        when(cond, remote(ref, ref, send_sem.at[i], result_sem.at[0, 0], (pair, sp)).wait_send)

    whole = near.at[:, :, :, PAIR, 0:tokens, :]
    part = near.at[:, :, :, PAIR, 0:half, :]
    drain(None, whole, 0)
    drain(has_outer, whole, 1)
    drain(has_far, whole, 2)
    for slot in slots:
        drain(both(has_up, held[slot]), part, 3 + slot)
        drain(both(has_down, held[slot]), part, 7 + slot)
    drain(None, results, 11)
    for j in heads:
        for goes, _, copy in stat_copies(j):
            when(goes, copy.wait_send)


def put_out(*refs):
    sources, targets, sems = refs[:4], refs[4:8], refs[8]
    copies = [pltpu.make_async_copy(sources[i], targets[i], sems.at[i]) for i in range(4)]
    for copy in copies:
        copy.start()
    for copy in copies:
        copy.wait()


def on_device(queries, key_vectors, values, grad_out, windows):
    local_shape = queries.shape
    row_count, col_count, features = local_shape[1:]
    head_count = windows.shape[1]
    head_size = features // head_count
    tokens = row_count * col_count
    mine = head_count // 2
    sizes = (
        head_count,
        head_size,
        row_count,
        col_count,
        lax.axis_size("tm"),
        lax.axis_size("space"),
    )
    flat = (tokens, features)
    low = jnp.bfloat16
    outs = pl.pallas_call(
        functools.partial(kernel, sizes),
        out_shape=[jax.ShapeDtypeStruct(flat, low)] * 4,
        in_specs=[pl.BlockSpec(memory_space=pltpu.HBM)] * 5,
        out_specs=[pl.BlockSpec(memory_space=pltpu.VMEM)] * 4,
        scratch_shapes=[
            pltpu.SMEM((2, head_count), jnp.int32),
            pltpu.VMEM((mine, tokens, 2 * tokens), jnp.float32),
            pltpu.VMEM((4 * mine, tokens, head_size), low),
            pltpu.VMEM((2, mine, 2, 4, 2 * tokens, head_size), low),
            pltpu.VMEM((4, mine, tokens, head_size), low),
            pltpu.VMEM((mine, 4, 8, tokens), jnp.float32),
            pltpu.VMEM((mine, 4, 8, tokens), jnp.float32),
            pltpu.VMEM((mine, 4, 8, tokens), jnp.float32),
            pltpu.SemaphoreType.DMA((4 * mine, 2)),
            pltpu.SemaphoreType.DMA,
            pltpu.SemaphoreType.DMA((12,)),
            pltpu.SemaphoreType.DMA((4 * mine, 3)),
            pltpu.SemaphoreType.DMA((2 * mine, 4, 2)),
            pltpu.SemaphoreType.DMA((4, mine)),
            pltpu.SemaphoreType.DMA((mine, 8)),
            pltpu.SemaphoreType.DMA((mine, 8)),
        ],
        compiler_params=pltpu.CompilerParams(
            collective_id=0, has_side_effects=True, vmem_limit_bytes=55_600_000
        ),
    )(
        windows,
        queries.reshape(flat),
        key_vectors.reshape(flat),
        values.reshape(flat),
        grad_out.reshape(flat),
    )
    outs = pl.pallas_call(
        put_out,
        out_shape=[jax.ShapeDtypeStruct(flat, low)] * 4,
        in_specs=[pl.BlockSpec(memory_space=pltpu.VMEM)] * 4,
        out_specs=[pl.BlockSpec(memory_space=pltpu.HBM)] * 4,
        scratch_shapes=[
            pltpu.SemaphoreType.DMA((4,)),
        ],
        compiler_params=pltpu.CompilerParams(vmem_limit_bytes=4_000_000),
    )(*outs)
    return tuple(out.reshape(local_shape) for out in outs)


def solution(mesh):
    spec = P("tm", "space", None, None)
    return jax.shard_map(
        on_device,
        mesh=mesh,
        in_specs=(spec, spec, spec, spec, P()),
        out_specs=(spec, spec, spec, spec),
        check_vma=False,
    )
```

time: 32.4 us -> 29.4 us (0.907)
  Pallas kernels: 30.5 us -> 27.8 us
    pallas_call x1, Pallas kernels: 29.6 us -> 26.9 us  [on_device(): pl.pallas_call(functools.partial(kernel, sizes), out_shape=[jax.ShapeDtyp...]
where the time goes in v2:
time: 29.4 us; the launch traced here: 29.1 us
  Pallas kernels  27.8 us (95%)
  local copies, waits for them, and re-layouts  0.67 us (2%)
  between operations  0.65 us (2%)
    pallas_call x1, Pallas kernels, on_device(): pl.pallas_call(functools.partial(kernel, sizes), out_shape=[jax.ShapeDtyp...  26.9 us
    pallas_call x1, Pallas kernels, on_device(): pl.pallas_call(put_out, out_shape=[jax.ShapeDtypeStruct(flat, low)] * 4,...  0.91 us
    unnamed x2, local copies, waits for them, and re-layouts  0.67 us

profile of v2, /device:TPU:0, one launch (start us, length us, event | category | flops | bytes accessed | tf_op | source)
XLA Modules:
  0.0 29.1 jit_solution(7414210971578660095)
XLA Ops:
  0.6 0.0 copy-start
  0.6 0.7 %copy-done = s32[2,6]{1,0:T(2,128)S(1)} copy-done((s32[2,6]{1,0:T(2,128)S(1)}, s32[2,6]{1,0:T(2,128)}, u32[]{:S(2)}) %copy-start) | copy-done | bytes 72
  1.3 26.9 %shard_map.84 = (bf16[128,768]{1,0:T(8,128)(2,1)S(1)}, bf16[128,768]{1,0:T(8,128)(2,1)S(1)}, bf16[128,768]{1,0:T(8,128)(2,1)S(1)}, bf16[128,768]{1,0:T(8,128)(2,1)S(1)}) custom-call(s32[2,6]{1,0:T(2,128)S(1)} %copy-done, bf16[128,768]{1,0:T(8,128)(2,1)} %bitcast.8, bf16[128,768]{1,0:T(8,128)(2,1)} %bitcast.9, bf16[128,768]{1,0:T(8,128)(2,1)} %bitcast.10, ...), custom_call_target="tpu_custom_call" | custom-call | tf_op jit(solution)/shard_map/pallas_call | solution.py:438
  28.2 0.9 %shard_map.85 = (bf16[128,768]{1,0:T(8,128)(2,1)}, bf16[128,768]{1,0:T(8,128)(2,1)}, bf16[128,768]{1,0:T(8,128)(2,1)}, bf16[128,768]{1,0:T(8,128)(2,1)}) custom-call(bf16[128,768]{1,0:T(8,128)(2,1)S(1)} %get-tuple-element.12.refs_0_, bf16[128,768]{1,0:T(8,128)(2,1)S(1)} %get-tuple-element.13.refs_1_, bf16[128,768]{1,0:T(8,128)(2,1)S(1)} %get-tuple-element.14.refs_2_, ...), custom_call_target="tpu_custom_call" | custom-call | tf_op jit(solution)/shard_map/pallas_call | solution.py:471
Async XLA Ops:
  0.6 0.7 %copy-start = (s32[2,6]{1,0:T(2,128)S(1)}, s32[2,6]{1,0:T(2,128)}, u32[]{:S(2)}) copy-start(s32[2,6]{1,0:T(2,128)} %win_hbm.1) | copy-start | bytes 148

commit v3 on v2

v3 whole, which is shorter than its diff:
```python
import functools
import math

import jax
import jax.numpy as jnp
from jax import lax
from jax.experimental import pallas as pl
from jax.experimental.pallas import tpu as pltpu
from jax.sharding import PartitionSpec as P

masked_score = -1e30
MESH = pl.DeviceIdType.MESH

OUTER, OWN, PAIR, FAR = range(4)

STAT_OWN, STAT_PAIR, STAT_OUTER, STAT_FAR = range(4)
ABOVE, BELOW = 4, 8

TO_PAIR, TO_FAR, TO_OUTER, RESULT, UP, DOWN, STAT = 0, 1, 2, 3, 4, 7, 10


def dot_nt(a, b):
    return lax.dot_general(a, b, (((1,), (1,)), ((), ())), preferred_element_type=jnp.float32)


def dot_nn(a, b):
    return lax.dot_general(a, b, (((1,), (0,)), ((), ())), preferred_element_type=jnp.float32)


def when(cond, action):
    if cond is None:
        action()
    else:
        pl.when(cond)(action)


def kernel(
    sizes,
    win_hbm,
    q_ref,
    k_ref,
    v_ref,
    g_ref,
    att_ref,
    gq_ref,
    gk_ref,
    gv_ref,
    win_ref,
    bias,
    near,
    results,
    stats,
    no_rows,
    no_stats,
    load_sem,
    send_sem,
    pair_sem,
    outer_sem,
    far_sem,
    halo_sem,
    stat_sem,
    result_sem,
):
    head_count, head_size, row_count, col_count, n_tm, n_space = sizes
    tokens = row_count * col_count
    half = tokens // 2
    mine = head_count // 2
    scale = 1.0 / math.sqrt(head_size)
    scale2 = scale * math.log2(math.e)
    tm, sp = lax.axis_index("tm"), lax.axis_index("space")
    side = lax.rem(tm, 2)
    pair = tm + 1 - 2 * side
    inner_to = tm + 2 - 4 * side
    outer_to = tm - 2 + 4 * side
    has_far = (inner_to >= 0) & (inner_to < n_tm)
    has_outer = (outer_to >= 0) & (outer_to < n_tm)
    has_up = sp > 0
    has_down = sp < n_space - 1
    heads = range(mine)
    pieces = [(phase, j, a) for phase in range(2) for j in heads for a in range(2)]
    ins = ((k_ref, v_ref), (q_ref, g_ref))
    outs = (att_ref, gq_ref, gk_ref, gv_ref)

    def head_cols(j, of_pair=False):
        first = (1 - side if of_pair else side) * mine + j
        return pl.ds(pl.multiple_of(first * head_size, head_size), head_size)

    barrier = pltpu.get_barrier_semaphore()

    def greet(cond, tm_to, sp_to):
        def signal():
            pl.semaphore_signal(barrier, inc=1, device_id=(tm_to, sp_to), device_id_type=MESH)

        when(cond, signal)

    greet(None, pair, sp)
    greet(has_far, inner_to, sp)
    greet(has_outer, outer_to, sp)
    greet(has_up, tm, sp - 1)
    greet(has_down, tm, sp + 1)

    def main_rows(i, slot):
        phase, j, a = pieces[i]
        return near.at[phase, j, a, slot, 0:tokens, :]

    def load(i):
        phase, j, a = pieces[i]
        return pltpu.make_async_copy(
            ins[phase][a].at[:, head_cols(j)], main_rows(i, OWN), load_sem.at[phase]
        )

    for i in range(len(pieces)):
        load(i).start()
    get_windows = pltpu.make_async_copy(win_hbm, win_ref, load_sem.at[2])
    get_windows.start()
    no_rows[...] = jnp.zeros_like(no_rows)
    no_stats[...] = jnp.zeros_like(no_stats)

    def remote(src, dst, send, recv, device):
        return pltpu.make_async_remote_copy(
            src_ref=src,
            dst_ref=dst,
            send_sem=send,
            recv_sem=recv,
            device_id=device,
            device_id_type=MESH,
        )

    def to_pair(i):
        phase, j, a = pieces[i]
        return remote(
            ins[phase][a].at[:, head_cols(j, True)],
            main_rows(i, PAIR),
            send_sem.at[TO_PAIR],
            pair_sem.at[i],
            (pair, sp),
        )

    def own_to_far(i):
        phase, j, a = pieces[i]
        return remote(
            main_rows(i, OWN),
            main_rows(i, FAR),
            send_sem.at[TO_FAR],
            far_sem.at[phase, j],
            (outer_to, sp),
        )

    def pair_to_outer(i):
        return remote(
            main_rows(i, PAIR),
            main_rows(i, OUTER),
            send_sem.at[TO_OUTER],
            outer_sem.at[i],
            (inner_to, sp),
        )

    def of_kind(slot):
        return {OUTER: 1, FAR: 2}.get(slot, 0)

    def halo_up(i, slot):
        phase, j, a = pieces[i]
        rows = near.at[phase, j, a, slot]
        return remote(
            rows.at[0:half, :],
            rows.at[tokens : tokens + half, :],
            send_sem.at[UP + of_kind(slot)],
            halo_sem.at[phase, j, of_kind(slot) % 2],
            (tm, sp - 1),
        )

    def halo_down(i, slot):
        phase, j, a = pieces[i]
        rows = near.at[phase, j, a, slot]
        return remote(
            rows.at[half:tokens, :],
            rows.at[tokens + half : 2 * tokens, :],
            send_sem.at[DOWN + of_kind(slot)],
            halo_sem.at[phase, j, of_kind(slot) % 2],
            (tm, sp + 1),
        )

    def halos(i, slot):
        when(has_up, lambda: halo_up(i, slot).start())
        when(has_down, lambda: halo_down(i, slot).start())

    expected = (
        1
        + has_far.astype(jnp.int32)
        + has_outer.astype(jnp.int32)
        + has_up.astype(jnp.int32)
        + has_down.astype(jnp.int32)
    )
    pl.semaphore_wait(barrier, expected)
    for i in range(len(pieces)):
        to_pair(i).start()
    for phase in range(2):
        rows = near.at[phase, :, :, OWN, 0:tokens, :]
        pltpu.make_async_copy(rows, rows, load_sem.at[phase]).wait()
        for i in range(len(pieces)):
            if pieces[i][0] == phase:
                when(has_outer, lambda: own_to_far(i).start())
                halos(i, OWN)

    def fill(source, target, sem):
        pltpu.make_async_copy(source, target, sem).start()

    def fill_side(first_row, first_stat):
        rows = slice(first_row, first_row + half)

        def all_frames():
            for phase in range(2):
                for j in heads:
                    at = near.at[phase, j, :, :, rows, :]
                    fill(no_rows.at[:, 0:1], at.at[:, 0:1], halo_sem.at[phase, j, 1])
                    fill(no_rows.at[:, 1:4], at.at[:, 1:4], halo_sem.at[phase, j, 0])
            for j in heads:
                fill(no_stats, stats.at[j, first_stat : first_stat + 4], stat_sem.at[j])

        def one_frame(slot, stat):
            for phase in range(2):
                for j in heads:
                    sem = halo_sem.at[phase, j, of_kind(slot) % 2]
                    fill(no_rows.at[:, slot], near.at[phase, j, :, slot, rows, :], sem)
            for j in heads:
                fill(no_stats.at[0], stats.at[j, first_stat + stat], stat_sem.at[j])

        return all_frames, one_frame

    for has_side, parts in (
        (has_down, fill_side(tokens, BELOW)),
        (has_up, fill_side(tokens + half, ABOVE)),
    ):
        all_frames, one_frame = parts
        pl.when(jnp.logical_not(has_side))(all_frames)
        no_outer, no_far = jnp.logical_not(has_outer), jnp.logical_not(has_far)
        pl.when(has_side & no_outer)(lambda: one_frame(OUTER, STAT_OUTER))
        pl.when(has_side & no_far)(lambda: one_frame(FAR, STAT_FAR))

    for has_frame, slot, stat in ((has_outer, OUTER, STAT_OUTER), (has_far, FAR, STAT_FAR)):

        @pl.when(jnp.logical_not(has_frame))
        def _():
            for phase in range(2):
                for j in heads:
                    near[phase, j, :, slot, 0:tokens, :] = jnp.zeros(
                        (2, tokens, head_size), near.dtype
                    )
            for j in heads:
                fill(no_stats.at[0], stats.at[j, stat], stat_sem.at[j])

    own_id = lax.broadcasted_iota(jnp.int32, (tokens, 2 * tokens), 0)
    near_id = lax.broadcasted_iota(jnp.int32, (tokens, 2 * tokens), 1)
    own_row, own_col = own_id // col_count, own_id % col_count
    near_row, near_col = near_id // col_count, near_id % col_count
    upper = near_row >= row_count + row_count // 2
    near_row = jnp.where(upper, near_row - 2 * row_count, near_row)
    global_row = sp * row_count + near_row
    row_inside = (global_row >= 0) & (global_row < n_space * row_count)
    row_gap = jnp.where(row_inside, jnp.abs(own_row - near_row), 1 << 20)
    col_gap = jnp.abs(own_col - near_col)

    get_windows.wait()
    for j in heads:
        h = side * mine + j
        inside = (row_gap <= win_ref[0, h]) & (col_gap <= win_ref[1, h])
        bias[j] = jnp.where(inside, 0.0, masked_score)

    def window(j, frame):
        here = bias[j]
        there = here + jnp.where(has_outer if frame == OWN else has_far, 0.0, masked_score)
        order = [there, here, here] if frame == OWN else [here, here, there]
        return jnp.concatenate(order, axis=1)

    def around(phase, j, a, frame):
        return near[phase, j, a, frame - 1 : frame + 2].reshape(6 * tokens, head_size)

    def put(kind, j, frame, value):
        if frame == OWN:
            outs[kind][:, head_cols(j)] = value
        else:
            results[kind, j] = value

    def give(kind, j):
        return remote(
            results.at[kind, j],
            outs[kind].at[:, head_cols(j)],
            send_sem.at[RESULT],
            result_sem,
            (pair, sp),
        )

    def forward(j, frame):
        query = near[1, j, 0, frame, 0:tokens, :]
        grad = near[1, j, 1, frame, 0:tokens, :]
        keys, vals = around(0, j, 0, frame), around(0, j, 1, frame)
        scores = dot_nt(query, keys) * scale2 + window(j, frame)
        top = jnp.max(scores, axis=1, keepdims=True)
        powers = jnp.exp2(scores - top)
        total = jnp.sum(powers, axis=1, keepdims=True)
        share = 1.0 / total
        attended = dot_nn(powers.astype(jnp.bfloat16), vals) * share
        put(0, j, frame, attended.astype(jnp.bfloat16))
        grad_weights = dot_nt(grad, vals)
        out_dot = jnp.sum(powers * grad_weights, axis=1, keepdims=True) * share
        grad_scores = (powers * (grad_weights - out_dot)).astype(jnp.bfloat16)
        put(1, j, frame, (dot_nn(grad_scores, keys) * (share * scale)).astype(jnp.bfloat16))
        return top + jnp.log2(total), out_dot

    row_lane = lax.broadcasted_iota(jnp.int32, (1, tokens), 1)

    def stat_row(j, r, frame):
        order = (STAT_OUTER, STAT_OWN, STAT_PAIR, STAT_FAR)
        parts = []
        for stat in order[frame - 1 : frame + 2]:
            parts.append(stats[j, stat, r : r + 1, :])
            down, up = stats[j, BELOW + stat, r : r + 1, :], stats[j, ABOVE + stat, r : r + 1, :]
            parts.append(jnp.where(row_lane < half, down, up))
        return jnp.concatenate(parts, axis=1)

    def backward(j, frame):
        key = near[0, j, 0, frame, 0:tokens, :]
        val = near[0, j, 1, frame, 0:tokens, :]
        queries, grads = around(1, j, 0, frame), around(1, j, 1, frame)
        scores = dot_nt(key, queries) * scale2 + window(j, frame)
        soft = jnp.exp2(scores - stat_row(j, 0, frame))
        put(3, j, frame, dot_nn(soft.astype(jnp.bfloat16), grads).astype(jnp.bfloat16))
        grad_scores = soft * (dot_nt(val, grads) - stat_row(j, 1, frame))
        key_sum = dot_nn(grad_scores.astype(jnp.bfloat16), queries)
        put(2, j, frame, (key_sum * scale).astype(jnp.bfloat16))

    def stat_copies(j):
        block = stats.at[j]
        found = [
            (has_far, STAT_PAIR, STAT_OUTER, 1, (inner_to, sp)),
            (has_outer, STAT_OWN, STAT_FAR, 1, (outer_to, sp)),
        ]
        for at, there, goes in ((BELOW, sp - 1, has_up), (ABOVE, sp + 1, has_down)):
            found += [
                (goes, STAT_OWN, at + STAT_OWN, 2, (tm, there)),
                (goes & has_far, STAT_PAIR, at + STAT_OUTER, 1, (inner_to, there)),
                (goes & has_outer, STAT_OWN, at + STAT_FAR, 1, (outer_to, there)),
            ]
        return [
            (
                goes,
                count,
                remote(
                    block.at[src : src + count],
                    block.at[dst : dst + count],
                    send_sem.at[STAT + n],
                    stat_sem.at[j],
                    device,
                ),
            )
            for n, (goes, src, dst, count, device) in enumerate(found)
        ]

    def step_pair_in(i):
        to_pair(i).wait_recv()
        when(has_far, lambda: pair_to_outer(i).start())
        halos(i, PAIR)

    def step_far_in(i):
        phase, j, _ = pieces[i]

        @pl.when(has_far)
        def _():
            rows = near.at[phase, j, :, FAR, 0:tokens, :]
            remote(rows, rows, send_sem.at[TO_FAR], far_sem.at[phase, j], (pair, sp)).wait_recv()
            for at in (i, i + 1):
                halos(at, FAR)

    def step_outer_in(i):
        @pl.when(has_outer)
        def _():
            pair_to_outer(i).wait_recv()
            halos(i, OUTER)

    def arrived(ref, sem):
        pltpu.make_async_copy(ref, ref, sem).wait()

    def arrive_halos(phase, j, outer):
        rows = slice(tokens, 2 * tokens)
        if outer:
            arrived(near.at[phase, j, :, OUTER, rows, :], halo_sem.at[phase, j, 1])
        else:
            arrived(near.at[phase, j, :, OWN : FAR + 1, rows, :], halo_sem.at[phase, j, 0])

    columns = {}

    def step_forward_pair(j):
        arrive_halos(0, j, False)
        columns[j] = forward(j, PAIR)
        for kind in (0, 1):
            give(kind, j).start()

    def step_forward_own(j):
        arrive_halos(0, j, True)
        found = (*forward(j, OWN), *columns.pop(j))
        lane = lax.broadcasted_iota(jnp.int32, (tokens, tokens), 1)
        spread = jnp.zeros((tokens, tokens), jnp.float32)
        for at, column in zip((0, 1, 8, 9), found, strict=True):
            spread = jnp.where(lane == at, column, spread)
        stats[j, STAT_OWN : STAT_PAIR + 1] = spread.T[0:16, :].reshape(2, 8, tokens)
        for goes, _, copy in stat_copies(j):
            when(goes, copy.start)

    def step_backward_pair(j):
        arrive_halos(1, j, False)
        arrived(stats.at[j, STAT_OUTER:], stat_sem.at[j])
        backward(j, PAIR)
        for kind in (2, 3):
            give(kind, j).start()

    def step_backward_own(j):
        arrive_halos(1, j, True)
        backward(j, OWN)

    times = []
    for i in range(len(pieces)):
        times.append((6.7 + 0.7 * i, step_pair_in, i))
        if pieces[i][2] == 0:
            times.append((7.41 + 0.7 * i, step_far_in, i))
        times.append((9.4 + 0.7 * i, step_outer_in, i))
    for j in heads:
        times.append((11.65 + 1.6 * j, step_forward_pair, j))
        times.append((12.45 + 1.6 * j, step_forward_own, j))
        times.append((16.4 + 1.15 * j, step_backward_pair, j))
        times.append((16.95 + 1.15 * j, step_backward_own, j))
    for _, step, index in sorted(times, key=lambda entry: entry[0]):
        step(index)

    remote(results, results, send_sem.at[RESULT], result_sem, (pair, sp)).wait()

    def drain(cond, ref, i):
        when(cond, remote(ref, ref, send_sem.at[i], result_sem, (pair, sp)).wait_send)

    whole = near.at[:, :, :, PAIR, 0:tokens, :]
    drain(None, whole, TO_PAIR)
    drain(has_outer, whole, TO_FAR)
    drain(has_far, whole, TO_OUTER)
    for first, cond in ((UP, has_up), (DOWN, has_down)):
        drain(cond, near.at[:, :, :, OWN : PAIR + 1, 0:half, :], first)
        drain(cond & has_outer, near.at[:, :, :, OUTER, 0:half, :], first + 1)
        drain(cond & has_far, near.at[:, :, :, FAR, 0:half, :], first + 2)
    for n, (goes, count, _) in enumerate(stat_copies(0)):
        drain(goes, stats.at[:, 0:count], STAT + n)


def put_out(*refs):
    sources, targets, sems = refs[:4], refs[4:8], refs[8]
    copies = [pltpu.make_async_copy(sources[i], targets[i], sems.at[i]) for i in range(4)]
    for copy in copies:
        copy.start()
    for copy in copies:
        copy.wait()


def on_device(queries, key_vectors, values, grad_out, windows):
    local_shape = queries.shape
    row_count, col_count, features = local_shape[1:]
    head_count = windows.shape[1]
    head_size = features // head_count
    tokens = row_count * col_count
    mine = head_count // 2
    half = tokens // 2
    sizes = (
        head_count,
        head_size,
        row_count,
        col_count,
        lax.axis_size("tm"),
        lax.axis_size("space"),
    )
    flat = (tokens, features)
    low = jnp.bfloat16
    outs = pl.pallas_call(
        functools.partial(kernel, sizes),
        out_shape=[jax.ShapeDtypeStruct(flat, low)] * 4,
        in_specs=[pl.BlockSpec(memory_space=pltpu.HBM)] * 5,
        out_specs=[pl.BlockSpec(memory_space=pltpu.VMEM)] * 4,
        scratch_shapes=[
            pltpu.SMEM((2, head_count), jnp.int32),
            pltpu.VMEM((mine, tokens, 2 * tokens), jnp.float32),
            pltpu.VMEM((2, mine, 2, 4, 2 * tokens, head_size), low),
            pltpu.VMEM((4, mine, tokens, head_size), low),
            pltpu.VMEM((mine, 12, 8, tokens), jnp.float32),
            pltpu.VMEM((2, 4, half, head_size), low),
            pltpu.VMEM((4, 8, tokens), jnp.float32),
            pltpu.SemaphoreType.DMA((3,)),
            pltpu.SemaphoreType.DMA((STAT + 8,)),
            pltpu.SemaphoreType.DMA((4 * mine,)),
            pltpu.SemaphoreType.DMA((4 * mine,)),
            pltpu.SemaphoreType.DMA((2, mine)),
            pltpu.SemaphoreType.DMA((2, mine, 2)),
            pltpu.SemaphoreType.DMA((mine,)),
            pltpu.SemaphoreType.DMA,
        ],
        compiler_params=pltpu.CompilerParams(
            collective_id=0, has_side_effects=True, vmem_limit_bytes=55_600_000
        ),
    )(
        pltpu.with_memory_space_constraint(windows, pltpu.HBM),
        queries.reshape(flat),
        key_vectors.reshape(flat),
        values.reshape(flat),
        grad_out.reshape(flat),
    )
    outs = pl.pallas_call(
        put_out,
        out_shape=[jax.ShapeDtypeStruct(flat, low)] * 4,
        in_specs=[pl.BlockSpec(memory_space=pltpu.VMEM)] * 4,
        out_specs=[pl.BlockSpec(memory_space=pltpu.HBM)] * 4,
        scratch_shapes=[
            pltpu.SemaphoreType.DMA((4,)),
        ],
        compiler_params=pltpu.CompilerParams(vmem_limit_bytes=4_000_000),
    )(*outs)
    return tuple(out.reshape(local_shape) for out in outs)


def solution(mesh):
    spec = P("tm", "space", None, None)
    return jax.shard_map(
        on_device,
        mesh=mesh,
        in_specs=(spec, spec, spec, spec, P()),
        out_specs=(spec, spec, spec, spec),
        check_vma=False,
    )
```

time: 29.4 us -> 28.1 us (0.956)
  local copies, waits for them, and re-layouts: 0.67 us -> 0 us
  Pallas kernels: 27.8 us -> 27.3 us
    unnamed x2 -> x0, local copies, waits for them, and re-layouts: 0.67 us -> none
    pallas_call x1, Pallas kernels: 26.9 us -> 26.4 us  [on_device(): pl.pallas_call(functools.partial(kernel, sizes), out_shape=[jax.ShapeDtyp...]
where the time goes in v3:
time: 28.1 us; the launch traced here: 27.9 us
  Pallas kernels  27.3 us (97%)
  between operations  0.64 us (2%)
    pallas_call x1, Pallas kernels, on_device(): pl.pallas_call(functools.partial(kernel, sizes), out_shape=[jax.ShapeDtyp...  26.4 us
    pallas_call x1, Pallas kernels, on_device(): pl.pallas_call(put_out, out_shape=[jax.ShapeDtypeStruct(flat, low)] * 4,...  0.91 us

profile of v3, /device:TPU:0, one launch (start us, length us, event | category | flops | bytes accessed | tf_op | source)
XLA Modules:
  0.0 27.9 jit_solution(15977266508014760784)
XLA Ops:
  0.6 26.4 %shard_map.84 = (bf16[128,768]{1,0:T(8,128)(2,1)S(1)}, bf16[128,768]{1,0:T(8,128)(2,1)S(1)}, bf16[128,768]{1,0:T(8,128)(2,1)S(1)}, bf16[128,768]{1,0:T(8,128)(2,1)S(1)}) custom-call(s32[2,6]{1,0:T(2,128)} %win_hbm.1, bf16[128,768]{1,0:T(8,128)(2,1)} %bitcast.8, bf16[128,768]{1,0:T(8,128)(2,1)} %bitcast.9, bf16[128,768]{1,0:T(8,128)(2,1)} %bitcast.10, ...), custom_call_target="tpu_custom_call" | custom-call | tf_op jit(solution)/shard_map/pallas_call | solution.py:478
  27.0 0.9 %shard_map.85 = (bf16[128,768]{1,0:T(8,128)(2,1)}, bf16[128,768]{1,0:T(8,128)(2,1)}, bf16[128,768]{1,0:T(8,128)(2,1)}, bf16[128,768]{1,0:T(8,128)(2,1)}) custom-call(bf16[128,768]{1,0:T(8,128)(2,1)S(1)} %get-tuple-element.12.refs_0_, bf16[128,768]{1,0:T(8,128)(2,1)S(1)} %get-tuple-element.13.refs_1_, bf16[128,768]{1,0:T(8,128)(2,1)S(1)} %get-tuple-element.14.refs_2_, ...), custom_call_target="tpu_custom_call" | custom-call | tf_op jit(solution)/shard_map/pallas_call | solution.py:510

commit v4 on v3

--- a/solution.py
+++ b/solution.py
@@ -50,6 +50,10 @@
     near,
     results,
     stats,
+    scores_ref,
+    grad_weights_ref,
+    powers_ref,
+    grad_scores_ref,
     no_rows,
     no_stats,
     load_sem,
@@ -194,7 +198,7 @@
     pl.semaphore_wait(barrier, expected)
     for i in range(len(pieces)):
         to_pair(i).start()
-    for phase in range(2):
+    def step_own_out(phase):
         rows = near.at[phase, :, :, OWN, 0:tokens, :]
         pltpu.make_async_copy(rows, rows, load_sem.at[phase]).wait()
         for i in range(len(pieces)):
@@ -306,6 +310,48 @@
         grad_scores = (powers * (grad_weights - out_dot)).astype(jnp.bfloat16)
         put(1, j, frame, (dot_nn(grad_scores, keys) * (share * scale)).astype(jnp.bfloat16))
         return top + jnp.log2(total), out_dot
+
+    def forward_both(j):
+        frames = slice(OWN, PAIR + 1)
+        own_rows, pair_rows = slice(0, tokens), slice(tokens, 2 * tokens)
+        side, middle = slice(0, 2 * tokens), slice(2 * tokens, 6 * tokens)
+        parts = ((own_rows, OUTER), (pair_rows, FAR))
+
+        def shared(a):
+            return near[0, j, a, frames].reshape(4 * tokens, head_size)
+
+        for a, out in ((0, scores_ref), (1, grad_weights_ref)):
+            rows = near[1, j, a, frames, 0:tokens, :].reshape(2 * tokens, head_size)
+            out[:, middle] = dot_nt(rows, shared(a))
+            for at, slot in parts:
+                out[at, side] = dot_nt(rows[at], near[0, j, a, slot])
+        shares, found = [], []
+        here = bias[j]
+        for at, held in ((own_rows, has_outer), (pair_rows, has_far)):
+            there = here + jnp.where(held, 0.0, masked_score)
+            window_bias = jnp.concatenate([there, here, here], axis=1)
+            scores = scores_ref[at] * scale2 + window_bias
+            top = jnp.max(scores, axis=1, keepdims=True)
+            powers = jnp.exp2(scores - top)
+            total = jnp.sum(powers, axis=1, keepdims=True)
+            share = 1.0 / total
+            powers_ref[at] = powers.astype(jnp.bfloat16)
+            grad_weights = grad_weights_ref[at]
+            out_dot = jnp.sum(powers * grad_weights, axis=1, keepdims=True) * share
+            grad_scores_ref[at] = (powers * (grad_weights - out_dot)).astype(jnp.bfloat16)
+            shares.append(share)
+            found += [top + jnp.log2(total), out_dot]
+        share = jnp.concatenate(shares, axis=0)
+        for kind, a, low, factor in (
+            (0, 1, powers_ref, share),
+            (1, 0, grad_scores_ref, share * scale),
+        ):
+            beside = [dot_nn(low[at, side], near[0, j, a, slot]) for at, slot in parts]
+            mixed = dot_nn(low[:, middle], shared(a)) + jnp.concatenate(beside, axis=0)
+            mixed = (mixed * factor).astype(jnp.bfloat16)
+            put(kind, j, PAIR, mixed[tokens:])
+            put(kind, j, OWN, mixed[:tokens])
+        return found
 
     row_lane = lax.broadcasted_iota(jnp.int32, (1, tokens), 1)
 
@@ -395,9 +441,7 @@
         for kind in (0, 1):
             give(kind, j).start()
 
-    def step_forward_own(j):
-        arrive_halos(0, j, True)
-        found = (*forward(j, OWN), *columns.pop(j))
+    def send_stats(j, found):
         lane = lax.broadcasted_iota(jnp.int32, (tokens, tokens), 1)
         spread = jnp.zeros((tokens, tokens), jnp.float32)
         for at, column in zip((0, 1, 8, 9), found, strict=True):
@@ -406,6 +450,18 @@
         for goes, _, copy in stat_copies(j):
             when(goes, copy.start)
 
+    def step_forward_own(j):
+        arrive_halos(0, j, True)
+        send_stats(j, (*forward(j, OWN), *columns.pop(j)))
+
+    def step_forward_both(j):
+        arrive_halos(0, j, False)
+        arrive_halos(0, j, True)
+        found = forward_both(j)
+        for kind in (0, 1):
+            give(kind, j).start()
+        send_stats(j, found)
+
     def step_backward_pair(j):
         arrive_halos(1, j, False)
         arrived(stats.at[j, STAT_OUTER:], stat_sem.at[j])
@@ -417,17 +473,21 @@
         arrive_halos(1, j, True)
         backward(j, OWN)
 
-    times = []
+    times = [(0.0, step_own_out, 0), (8.0, step_own_out, 1)]
     for i in range(len(pieces)):
-        times.append((6.7 + 0.7 * i, step_pair_in, i))
+        times.append((6.15 + 0.7 * i, step_pair_in, i))
         if pieces[i][2] == 0:
-            times.append((7.41 + 0.7 * i, step_far_in, i))
-        times.append((9.4 + 0.7 * i, step_outer_in, i))
+            times.append((6.9 + 0.7 * i, step_far_in, i))
+        late = 4.0 if i >= len(pieces) - 2 else 0.0
+        times.append((8.75 + 0.7 * i + late, step_outer_in, i))
     for j in heads:
-        times.append((11.65 + 1.6 * j, step_forward_pair, j))
-        times.append((12.45 + 1.6 * j, step_forward_own, j))
-        times.append((16.4 + 1.15 * j, step_backward_pair, j))
-        times.append((16.95 + 1.15 * j, step_backward_own, j))
+        if j == 0:
+            times.append((11.06, step_forward_pair, j))
+            times.append((12.5, step_forward_own, j))
+        else:
+            times.append((11.5 + 1.4 * j, step_forward_both, j))
+        times.append((15.5 + 1.05 * j, step_backward_pair, j))
+        times.append((16.5 + (4.5 + 0.5 * j if j > 0 else 0.0), step_backward_own, j))
     for _, step, index in sorted(times, key=lambda entry: entry[0]):
         step(index)
 
@@ -486,6 +546,10 @@
             pltpu.VMEM((2, mine, 2, 4, 2 * tokens, head_size), low),
             pltpu.VMEM((4, mine, tokens, head_size), low),
             pltpu.VMEM((mine, 12, 8, tokens), jnp.float32),
+            pltpu.VMEM((2 * tokens, 6 * tokens), jnp.float32),
+            pltpu.VMEM((2 * tokens, 6 * tokens), jnp.float32),
+            pltpu.VMEM((2 * tokens, 6 * tokens), low),
+            pltpu.VMEM((2 * tokens, 6 * tokens), low),
             pltpu.VMEM((2, 4, half, head_size), low),
             pltpu.VMEM((4, 8, tokens), jnp.float32),
             pltpu.SemaphoreType.DMA((3,)),

time: 28.1 us -> 27.8 us (0.989)
  Pallas kernels: 27.3 us -> 27 us
    pallas_call x1, Pallas kernels: 26.4 us -> 26.1 us  [on_device(): pl.pallas_call(functools.partial(kernel, sizes), out_shape=[jax.ShapeDtyp...]
where the time goes in v4:
time: 27.8 us; the launch traced here: 27.6 us
  Pallas kernels  27 us (97%)
  between operations  0.64 us (2%)
    pallas_call x1, Pallas kernels, on_device(): pl.pallas_call(functools.partial(kernel, sizes), out_shape=[jax.ShapeDtyp...  26.1 us
    pallas_call x1, Pallas kernels, on_device(): pl.pallas_call(put_out, out_shape=[jax.ShapeDtypeStruct(flat, low)] * 4,...  0.91 us

profile of v4, /device:TPU:0, one launch (start us, length us, event | category | flops | bytes accessed | tf_op | source)
XLA Modules:
  0.0 27.6 jit_solution(11110886196792537967)
XLA Ops:
  0.6 26.1 %shard_map.84 = (bf16[128,768]{1,0:T(8,128)(2,1)S(1)}, bf16[128,768]{1,0:T(8,128)(2,1)S(1)}, bf16[128,768]{1,0:T(8,128)(2,1)S(1)}, bf16[128,768]{1,0:T(8,128)(2,1)S(1)}) custom-call(s32[2,6]{1,0:T(2,128)} %win_hbm.1, bf16[128,768]{1,0:T(8,128)(2,1)} %bitcast.8, bf16[128,768]{1,0:T(8,128)(2,1)} %bitcast.9, bf16[128,768]{1,0:T(8,128)(2,1)} %bitcast.10, ...), custom_call_target="tpu_custom_call" | custom-call | tf_op jit(solution)/shard_map/pallas_call | solution.py:538
  26.7 0.9 %shard_map.85 = (bf16[128,768]{1,0:T(8,128)(2,1)}, bf16[128,768]{1,0:T(8,128)(2,1)}, bf16[128,768]{1,0:T(8,128)(2,1)}, bf16[128,768]{1,0:T(8,128)(2,1)}) custom-call(bf16[128,768]{1,0:T(8,128)(2,1)S(1)} %get-tuple-element.12.refs_0_, bf16[128,768]{1,0:T(8,128)(2,1)S(1)} %get-tuple-element.13.refs_1_, bf16[128,768]{1,0:T(8,128)(2,1)S(1)} %get-tuple-element.14.refs_2_, ...), custom_call_target="tpu_custom_call" | custom-call | tf_op jit(solution)/shard_map/pallas_call | solution.py:574

commit v5 on v4

--- a/solution.py
+++ b/solution.py
@@ -341,6 +341,7 @@
             grad_scores_ref[at] = (powers * (grad_weights - out_dot)).astype(jnp.bfloat16)
             shares.append(share)
             found += [top + jnp.log2(total), out_dot]
+        send_stats(j, found)
         share = jnp.concatenate(shares, axis=0)
         for kind, a, low, factor in (
             (0, 1, powers_ref, share),
@@ -351,7 +352,6 @@
             mixed = (mixed * factor).astype(jnp.bfloat16)
             put(kind, j, PAIR, mixed[tokens:])
             put(kind, j, OWN, mixed[:tokens])
-        return found
 
     row_lane = lax.broadcasted_iota(jnp.int32, (1, tokens), 1)
 
@@ -364,15 +364,23 @@
             parts.append(jnp.where(row_lane < half, down, up))
         return jnp.concatenate(parts, axis=1)
 
-    def backward(j, frame):
+    def backward_rows(frame):
+        return slice((frame - OWN) * tokens, (frame - OWN + 1) * tokens)
+
+    def backward_start(j, frame):
+        at = backward_rows(frame)
         key = near[0, j, 0, frame, 0:tokens, :]
         val = near[0, j, 1, frame, 0:tokens, :]
-        queries, grads = around(1, j, 0, frame), around(1, j, 1, frame)
-        scores = dot_nt(key, queries) * scale2 + window(j, frame)
-        soft = jnp.exp2(scores - stat_row(j, 0, frame))
-        put(3, j, frame, dot_nn(soft.astype(jnp.bfloat16), grads).astype(jnp.bfloat16))
-        grad_scores = soft * (dot_nt(val, grads) - stat_row(j, 1, frame))
-        key_sum = dot_nn(grad_scores.astype(jnp.bfloat16), queries)
+        scores_ref[at] = dot_nt(key, around(1, j, 0, frame)) * scale2 + window(j, frame)
+        grad_weights_ref[at] = dot_nt(val, around(1, j, 1, frame))
+
+    def backward(j, frame):
+        at = backward_rows(frame)
+        soft = jnp.exp2(scores_ref[at] - stat_row(j, 0, frame))
+        grad_scores = soft * (grad_weights_ref[at] - stat_row(j, 1, frame))
+        value_sum = dot_nn(soft.astype(jnp.bfloat16), around(1, j, 1, frame))
+        put(3, j, frame, value_sum.astype(jnp.bfloat16))
+        key_sum = dot_nn(grad_scores.astype(jnp.bfloat16), around(1, j, 0, frame))
         put(2, j, frame, (key_sum * scale).astype(jnp.bfloat16))
 
     def stat_copies(j):
@@ -457,20 +465,21 @@
     def step_forward_both(j):
         arrive_halos(0, j, False)
         arrive_halos(0, j, True)
-        found = forward_both(j)
+        forward_both(j)
         for kind in (0, 1):
             give(kind, j).start()
-        send_stats(j, found)
 
     def step_backward_pair(j):
         arrive_halos(1, j, False)
+        backward_start(j, PAIR)
         arrived(stats.at[j, STAT_OUTER:], stat_sem.at[j])
         backward(j, PAIR)
-        for kind in (2, 3):
+        for kind in (3, 2):
             give(kind, j).start()
 
     def step_backward_own(j):
         arrive_halos(1, j, True)
+        backward_start(j, OWN)
         backward(j, OWN)
 
     times = [(0.0, step_own_out, 0), (8.0, step_own_out, 1)]

time: 27.8 us -> 27.4 us (0.986)
  Pallas kernels: 27 us -> 26.6 us
    pallas_call x1, Pallas kernels: 26.1 us -> 25.7 us  [on_device(): pl.pallas_call(functools.partial(kernel, sizes), out_shape=[jax.ShapeDtyp...]
where the time goes in v5:
time: 27.4 us; the launch traced here: 27.2 us
  Pallas kernels  26.6 us (97%)
  between operations  0.64 us (2%)
    pallas_call x1, Pallas kernels, on_device(): pl.pallas_call(functools.partial(kernel, sizes), out_shape=[jax.ShapeDtyp...  25.7 us
    pallas_call x1, Pallas kernels, on_device(): pl.pallas_call(put_out, out_shape=[jax.ShapeDtypeStruct(flat, low)] * 4,...  0.91 us

profile of v5, /device:TPU:0, one launch (start us, length us, event | category | flops | bytes accessed | tf_op | source)
XLA Modules:
  0.0 27.2 jit_solution(17366243443266875776)
XLA Ops:
  0.6 25.7 %shard_map.84 = (bf16[128,768]{1,0:T(8,128)(2,1)S(1)}, bf16[128,768]{1,0:T(8,128)(2,1)S(1)}, bf16[128,768]{1,0:T(8,128)(2,1)S(1)}, bf16[128,768]{1,0:T(8,128)(2,1)S(1)}) custom-call(s32[2,6]{1,0:T(2,128)} %win_hbm.1, bf16[128,768]{1,0:T(8,128)(2,1)} %bitcast.8, bf16[128,768]{1,0:T(8,128)(2,1)} %bitcast.9, bf16[128,768]{1,0:T(8,128)(2,1)} %bitcast.10, ...), custom_call_target="tpu_custom_call" | custom-call | tf_op jit(solution)/shard_map/pallas_call | solution.py:547
  26.3 0.9 %shard_map.85 = (bf16[128,768]{1,0:T(8,128)(2,1)}, bf16[128,768]{1,0:T(8,128)(2,1)}, bf16[128,768]{1,0:T(8,128)(2,1)}, bf16[128,768]{1,0:T(8,128)(2,1)}) custom-call(bf16[128,768]{1,0:T(8,128)(2,1)S(1)} %get-tuple-element.12.refs_0_, bf16[128,768]{1,0:T(8,128)(2,1)S(1)} %get-tuple-element.13.refs_1_, bf16[128,768]{1,0:T(8,128)(2,1)S(1)} %get-tuple-element.14.refs_2_, ...), custom_call_target="tpu_custom_call" | custom-call | tf_op jit(solution)/shard_map/pallas_call | solution.py:583

commit v6 on v3

--- a/solution.py
+++ b/solution.py
@@ -13,7 +13,7 @@
 
 OUTER, OWN, PAIR, FAR = range(4)
 
-STAT_OWN, STAT_PAIR, STAT_OUTER, STAT_FAR = range(4)
+STAT_OWN, STAT_PAIR, STAT_FAR, STAT_OUTER = range(4)
 ABOVE, BELOW = 4, 8
 
 TO_PAIR, TO_FAR, TO_OUTER, RESULT, UP, DOWN, STAT = 0, 1, 2, 3, 4, 7, 10
@@ -50,6 +50,10 @@
     near,
     results,
     stats,
+    scores_ref,
+    grad_weights_ref,
+    powers_ref,
+    grad_scores_ref,
     no_rows,
     no_stats,
     load_sem,
@@ -77,7 +81,9 @@
     has_up = sp > 0
     has_down = sp < n_space - 1
     heads = range(mine)
-    pieces = [(phase, j, a) for phase in range(2) for j in heads for a in range(2)]
+    blocks = [(phase, j) for phase in range(2) for j in heads]
+    blocks.insert(mine - 1, blocks.pop(mine))
+    pieces = [(phase, j, a) for phase, j in blocks for a in range(2)]
     ins = ((k_ref, v_ref), (q_ref, g_ref))
     outs = (att_ref, gq_ref, gk_ref, gv_ref)
 
@@ -194,7 +200,7 @@
     pl.semaphore_wait(barrier, expected)
     for i in range(len(pieces)):
         to_pair(i).start()
-    for phase in range(2):
+    def step_own_out(phase):
         rows = near.at[phase, :, :, OWN, 0:tokens, :]
         pltpu.make_async_copy(rows, rows, load_sem.at[phase]).wait()
         for i in range(len(pieces)):
@@ -215,7 +221,9 @@
                     fill(no_rows.at[:, 0:1], at.at[:, 0:1], halo_sem.at[phase, j, 1])
                     fill(no_rows.at[:, 1:4], at.at[:, 1:4], halo_sem.at[phase, j, 0])
             for j in heads:
-                fill(no_stats, stats.at[j, first_stat : first_stat + 4], stat_sem.at[j])
+                last = first_stat + STAT_OUTER
+                fill(no_stats.at[0:3], stats.at[j, first_stat:last], stat_sem.at[j, 0])
+                fill(no_stats.at[3], stats.at[j, last], stat_sem.at[j, 1])
 
         def one_frame(slot, stat):
             for phase in range(2):
@@ -223,7 +231,8 @@
                     sem = halo_sem.at[phase, j, of_kind(slot) % 2]
                     fill(no_rows.at[:, slot], near.at[phase, j, :, slot, rows, :], sem)
             for j in heads:
-                fill(no_stats.at[0], stats.at[j, first_stat + stat], stat_sem.at[j])
+                sem = stat_sem.at[j, stat // STAT_OUTER]
+                fill(no_stats.at[0], stats.at[j, first_stat + stat], sem)
 
         return all_frames, one_frame
 
@@ -247,7 +256,7 @@
                         (2, tokens, head_size), near.dtype
                     )
             for j in heads:
-                fill(no_stats.at[0], stats.at[j, stat], stat_sem.at[j])
+                fill(no_stats.at[0], stats.at[j, stat], stat_sem.at[j, stat // STAT_OUTER])
 
     own_id = lax.broadcasted_iota(jnp.int32, (tokens, 2 * tokens), 0)
     near_id = lax.broadcasted_iota(jnp.int32, (tokens, 2 * tokens), 1)
@@ -291,22 +300,27 @@
         )
 
     def forward(j, frame):
-        query = near[1, j, 0, frame, 0:tokens, :]
-        grad = near[1, j, 1, frame, 0:tokens, :]
-        keys, vals = around(0, j, 0, frame), around(0, j, 1, frame)
-        scores = dot_nt(query, keys) * scale2 + window(j, frame)
+        at = slice((frame - OWN) * tokens, (frame - OWN + 1) * tokens)
+        scores_ref[at] = dot_nt(near[1, j, 0, frame, 0:tokens, :], around(0, j, 0, frame))
+        grad_weights_ref[at] = dot_nt(near[1, j, 1, frame, 0:tokens, :], around(0, j, 1, frame))
+        scores = scores_ref[at] * scale2 + window(j, frame)
         top = jnp.max(scores, axis=1, keepdims=True)
         powers = jnp.exp2(scores - top)
         total = jnp.sum(powers, axis=1, keepdims=True)
         share = 1.0 / total
-        attended = dot_nn(powers.astype(jnp.bfloat16), vals) * share
+        powers_ref[at] = powers.astype(jnp.bfloat16)
+        grad_weights = grad_weights_ref[at]
+        out_dot = jnp.sum(powers * grad_weights, axis=1, keepdims=True) * share
+        grad_scores_ref[at] = (powers * (grad_weights - out_dot)).astype(jnp.bfloat16)
+        found = (top + jnp.log2(total), out_dot)
+        if frame == PAIR:
+            columns[j] = found
+        else:
+            send_stats(j, (*found, *columns.pop(j)))
+        attended = dot_nn(powers_ref[at], around(0, j, 1, frame)) * share
         put(0, j, frame, attended.astype(jnp.bfloat16))
-        grad_weights = dot_nt(grad, vals)
-        out_dot = jnp.sum(powers * grad_weights, axis=1, keepdims=True) * share
-        grad_scores = (powers * (grad_weights - out_dot)).astype(jnp.bfloat16)
-        put(1, j, frame, (dot_nn(grad_scores, keys) * (share * scale)).astype(jnp.bfloat16))
-        return top + jnp.log2(total), out_dot
-
+        query_sum = dot_nn(grad_scores_ref[at], around(0, j, 0, frame)) * (share * scale)
+        put(1, j, frame, query_sum.astype(jnp.bfloat16))
     row_lane = lax.broadcasted_iota(jnp.int32, (1, tokens), 1)
 
     def stat_row(j, r, frame):
@@ -318,15 +332,23 @@
             parts.append(jnp.where(row_lane < half, down, up))
         return jnp.concatenate(parts, axis=1)
 
-    def backward(j, frame):
+    def backward_rows(frame):
+        return slice((frame - OWN) * tokens, (frame - OWN + 1) * tokens)
+
+    def backward_start(j, frame):
+        at = backward_rows(frame)
         key = near[0, j, 0, frame, 0:tokens, :]
         val = near[0, j, 1, frame, 0:tokens, :]
-        queries, grads = around(1, j, 0, frame), around(1, j, 1, frame)
-        scores = dot_nt(key, queries) * scale2 + window(j, frame)
-        soft = jnp.exp2(scores - stat_row(j, 0, frame))
-        put(3, j, frame, dot_nn(soft.astype(jnp.bfloat16), grads).astype(jnp.bfloat16))
-        grad_scores = soft * (dot_nt(val, grads) - stat_row(j, 1, frame))
-        key_sum = dot_nn(grad_scores.astype(jnp.bfloat16), queries)
+        scores_ref[at] = dot_nt(key, around(1, j, 0, frame)) * scale2 + window(j, frame)
+        grad_weights_ref[at] = dot_nt(val, around(1, j, 1, frame))
+
+    def backward(j, frame):
+        at = backward_rows(frame)
+        soft = jnp.exp2(scores_ref[at] - stat_row(j, 0, frame))
+        grad_scores = soft * (grad_weights_ref[at] - stat_row(j, 1, frame))
+        value_sum = dot_nn(soft.astype(jnp.bfloat16), around(1, j, 1, frame))
+        put(3, j, frame, value_sum.astype(jnp.bfloat16))
+        key_sum = dot_nn(grad_scores.astype(jnp.bfloat16), around(1, j, 0, frame))
         put(2, j, frame, (key_sum * scale).astype(jnp.bfloat16))
 
     def stat_copies(j):
@@ -349,7 +371,7 @@
                     block.at[src : src + count],
                     block.at[dst : dst + count],
                     send_sem.at[STAT + n],
-                    stat_sem.at[j],
+                    stat_sem.at[j, dst % 4 // STAT_OUTER],
                     device,
                 ),
             )
@@ -391,13 +413,11 @@
 
     def step_forward_pair(j):
         arrive_halos(0, j, False)
-        columns[j] = forward(j, PAIR)
+        forward(j, PAIR)
         for kind in (0, 1):
             give(kind, j).start()
 
-    def step_forward_own(j):
-        arrive_halos(0, j, True)
-        found = (*forward(j, OWN), *columns.pop(j))
+    def send_stats(j, found):
         lane = lax.broadcasted_iota(jnp.int32, (tokens, tokens), 1)
         spread = jnp.zeros((tokens, tokens), jnp.float32)
         for at, column in zip((0, 1, 8, 9), found, strict=True):
@@ -406,28 +426,39 @@
         for goes, _, copy in stat_copies(j):
             when(goes, copy.start)
 
+    def step_forward_own(j):
+        arrive_halos(0, j, True)
+        forward(j, OWN)
+
     def step_backward_pair(j):
         arrive_halos(1, j, False)
-        arrived(stats.at[j, STAT_OUTER:], stat_sem.at[j])
+        backward_start(j, PAIR)
+        arrived(stats.at[j, 0:7], stat_sem.at[j, 0])
         backward(j, PAIR)
-        for kind in (2, 3):
+        for kind in (3, 2):
             give(kind, j).start()
 
     def step_backward_own(j):
         arrive_halos(1, j, True)
+        backward_start(j, OWN)
+        arrived(stats.at[j, 0:3], stat_sem.at[j, 1])
         backward(j, OWN)
 
-    times = []
-    for i in range(len(pieces)):
-        times.append((6.7 + 0.7 * i, step_pair_in, i))
-        if pieces[i][2] == 0:
-            times.append((7.41 + 0.7 * i, step_far_in, i))
-        times.append((9.4 + 0.7 * i, step_outer_in, i))
+    times = [(0.0, step_own_out, 0), (7.5, step_own_out, 1)]
+    for i, (phase, j, a) in enumerate(pieces):
+        times.append((6.15 + 0.7 * i, step_pair_in, i))
+        if a == 0:
+            at = 6.9 + 0.7 * i if phase == 0 else (11.85 if j == 0 else 14.46)
+            times.append((at, step_far_in, i))
+        late = 0.0
+        if phase == 1:
+            late = 2.2 if j == 0 else (0.25 if j == mine - 1 else 0.0)
+        times.append((8.75 + 0.7 * i + late, step_outer_in, i))
     for j in heads:
-        times.append((11.65 + 1.6 * j, step_forward_pair, j))
-        times.append((12.45 + 1.6 * j, step_forward_own, j))
-        times.append((16.4 + 1.15 * j, step_backward_pair, j))
-        times.append((16.95 + 1.15 * j, step_backward_own, j))
+        times.append((9.66 if j == 0 else 11.1 + 1.4 * j, step_forward_pair, j))
+        times.append((13.1 + 1.4 * j if j == mine - 1 else 11.5 + 2.2 * j, step_forward_own, j))
+        times.append((15.0 + 1.6 * j, step_backward_pair, j))
+        times.append((16.75 + (4.5 + 0.5 * j if j > 0 else 0.0), step_backward_own, j))
     for _, step, index in sorted(times, key=lambda entry: entry[0]):
         step(index)
 
@@ -486,6 +517,10 @@
             pltpu.VMEM((2, mine, 2, 4, 2 * tokens, head_size), low),
             pltpu.VMEM((4, mine, tokens, head_size), low),
             pltpu.VMEM((mine, 12, 8, tokens), jnp.float32),
+            pltpu.VMEM((2 * tokens, 6 * tokens), jnp.float32),
+            pltpu.VMEM((2 * tokens, 6 * tokens), jnp.float32),
+            pltpu.VMEM((2 * tokens, 6 * tokens), low),
+            pltpu.VMEM((2 * tokens, 6 * tokens), low),
             pltpu.VMEM((2, 4, half, head_size), low),
             pltpu.VMEM((4, 8, tokens), jnp.float32),
             pltpu.SemaphoreType.DMA((3,)),
@@ -494,7 +529,7 @@
             pltpu.SemaphoreType.DMA((4 * mine,)),
             pltpu.SemaphoreType.DMA((2, mine)),
             pltpu.SemaphoreType.DMA((2, mine, 2)),
-            pltpu.SemaphoreType.DMA((mine,)),
+            pltpu.SemaphoreType.DMA((mine, 2)),
             pltpu.SemaphoreType.DMA,
         ],
         compiler_params=pltpu.CompilerParams(

time: 28.1 us -> 26.8 us (0.954)
  Pallas kernels: 27.3 us -> 26 us
    pallas_call x1, Pallas kernels: 26.4 us -> 25 us  [on_device(): pl.pallas_call(functools.partial(kernel, sizes), out_shape=[jax.ShapeDtyp...]
where the time goes in v6:
time: 26.8 us; the launch traced here: 26.6 us
  Pallas kernels  26 us (97%)
  between operations  0.64 us (2%)
    pallas_call x1, Pallas kernels, on_device(): pl.pallas_call(functools.partial(kernel, sizes), out_shape=[jax.ShapeDtyp...  25 us
    pallas_call x1, Pallas kernels, on_device(): pl.pallas_call(put_out, out_shape=[jax.ShapeDtypeStruct(flat, low)] * 4,...  0.91 us

profile of v6, /device:TPU:0, one launch (start us, length us, event | category | flops | bytes accessed | tf_op | source)
XLA Modules:
  0.0 26.6 jit_solution(3404661480593490496)
XLA Ops:
  0.6 25.0 %shard_map.84 = (bf16[128,768]{1,0:T(8,128)(2,1)S(1)}, bf16[128,768]{1,0:T(8,128)(2,1)S(1)}, bf16[128,768]{1,0:T(8,128)(2,1)S(1)}, bf16[128,768]{1,0:T(8,128)(2,1)S(1)}) custom-call(s32[2,6]{1,0:T(2,128)} %win_hbm.1, bf16[128,768]{1,0:T(8,128)(2,1)} %bitcast.8, bf16[128,768]{1,0:T(8,128)(2,1)} %bitcast.9, bf16[128,768]{1,0:T(8,128)(2,1)} %bitcast.10, ...), custom_call_target="tpu_custom_call" | custom-call | tf_op jit(solution)/shard_map/pallas_call | solution.py:509
  25.7 0.9 %shard_map.85 = (bf16[128,768]{1,0:T(8,128)(2,1)}, bf16[128,768]{1,0:T(8,128)(2,1)}, bf16[128,768]{1,0:T(8,128)(2,1)}, bf16[128,768]{1,0:T(8,128)(2,1)}) custom-call(bf16[128,768]{1,0:T(8,128)(2,1)S(1)} %get-tuple-element.12.refs_0_, bf16[128,768]{1,0:T(8,128)(2,1)S(1)} %get-tuple-element.13.refs_1_, bf16[128,768]{1,0:T(8,128)(2,1)S(1)} %get-tuple-element.14.refs_2_, ...), custom_call_target="tpu_custom_call" | custom-call | tf_op jit(solution)/shard_map/pallas_call | solution.py:545

commit v7 on v6

--- a/solution.py
+++ b/solution.py
@@ -81,9 +81,7 @@
     has_up = sp > 0
     has_down = sp < n_space - 1
     heads = range(mine)
-    blocks = [(phase, j) for phase in range(2) for j in heads]
-    blocks.insert(mine - 1, blocks.pop(mine))
-    pieces = [(phase, j, a) for phase, j in blocks for a in range(2)]
+    pieces = [(phase, j, a) for phase in range(2) for j in heads for a in range(2)]
     ins = ((k_ref, v_ref), (q_ref, g_ref))
     outs = (att_ref, gq_ref, gk_ref, gv_ref)
 
@@ -206,6 +204,12 @@
         for i in range(len(pieces)):
             if pieces[i][0] == phase:
                 when(has_outer, lambda: own_to_far(i).start())
+                if phase == 0:
+                    halos(i, OWN)
+
+    def step_own_halo(j):
+        for i in range(len(pieces)):
+            if pieces[i][:2] == (1, j):
                 halos(i, OWN)
 
     def fill(source, target, sem):
@@ -448,17 +452,15 @@
     for i, (phase, j, a) in enumerate(pieces):
         times.append((6.15 + 0.7 * i, step_pair_in, i))
         if a == 0:
-            at = 6.9 + 0.7 * i if phase == 0 else (11.85 if j == 0 else 14.46)
+            at = 6.9 + 0.7 * i if phase == 0 else (12.6 if j == 0 else 14.0)
             times.append((at, step_far_in, i))
-        late = 0.0
-        if phase == 1:
-            late = 2.2 if j == 0 else (0.25 if j == mine - 1 else 0.0)
-        times.append((8.75 + 0.7 * i + late, step_outer_in, i))
+        times.append((8.75 + 0.7 * i + phase, step_outer_in, i))
     for j in heads:
-        times.append((9.66 if j == 0 else 11.1 + 1.4 * j, step_forward_pair, j))
-        times.append((13.1 + 1.4 * j if j == mine - 1 else 11.5 + 2.2 * j, step_forward_own, j))
-        times.append((15.0 + 1.6 * j, step_backward_pair, j))
-        times.append((16.75 + (4.5 + 0.5 * j if j > 0 else 0.0), step_backward_own, j))
+        times.append((7.55 + 2.8 * j, step_own_halo, j))
+        times.append((11.06 + 1.42 * j, step_forward_pair, j))
+        times.append((11.35 + 1.8 * j, step_forward_own, j))
+        times.append((15.0 + 1.5 * j, step_backward_pair, j))
+        times.append((16.6 + (4.5 + 0.5 * j if j > 0 else 0.0), step_backward_own, j))
     for _, step, index in sorted(times, key=lambda entry: entry[0]):
         step(index)
 

time: 26.8 us -> 26.2 us (0.978)
  Pallas kernels: 26 us -> 25.5 us
    pallas_call x1, Pallas kernels: 25 us -> 24.5 us  [on_device(): pl.pallas_call(functools.partial(kernel, sizes), out_shape=[jax.ShapeDtyp...]
where the time goes in v7:
time: 26.2 us; the launch traced here: 26.1 us
  Pallas kernels  25.5 us (97%)
  between operations  0.64 us (2%)
    pallas_call x1, Pallas kernels, on_device(): pl.pallas_call(functools.partial(kernel, sizes), out_shape=[jax.ShapeDtyp...  24.5 us
    pallas_call x1, Pallas kernels, on_device(): pl.pallas_call(put_out, out_shape=[jax.ShapeDtypeStruct(flat, low)] * 4,...  0.91 us

profile of v7, /device:TPU:0, one launch (start us, length us, event | category | flops | bytes accessed | tf_op | source)
XLA Modules:
  0.0 26.1 jit_solution(14861368839446728744)
XLA Ops:
  0.6 24.5 %shard_map.84 = (bf16[128,768]{1,0:T(8,128)(2,1)S(1)}, bf16[128,768]{1,0:T(8,128)(2,1)S(1)}, bf16[128,768]{1,0:T(8,128)(2,1)S(1)}, bf16[128,768]{1,0:T(8,128)(2,1)S(1)}) custom-call(s32[2,6]{1,0:T(2,128)} %win_hbm.1, bf16[128,768]{1,0:T(8,128)(2,1)} %bitcast.8, bf16[128,768]{1,0:T(8,128)(2,1)} %bitcast.9, bf16[128,768]{1,0:T(8,128)(2,1)} %bitcast.10, ...), custom_call_target="tpu_custom_call" | custom-call | tf_op jit(solution)/shard_map/pallas_call | solution.py:511
  25.2 0.9 %shard_map.85 = (bf16[128,768]{1,0:T(8,128)(2,1)}, bf16[128,768]{1,0:T(8,128)(2,1)}, bf16[128,768]{1,0:T(8,128)(2,1)}, bf16[128,768]{1,0:T(8,128)(2,1)}) custom-call(bf16[128,768]{1,0:T(8,128)(2,1)S(1)} %get-tuple-element.12.refs_0_, bf16[128,768]{1,0:T(8,128)(2,1)S(1)} %get-tuple-element.13.refs_1_, bf16[128,768]{1,0:T(8,128)(2,1)S(1)} %get-tuple-element.14.refs_2_, ...), custom_call_target="tpu_custom_call" | custom-call | tf_op jit(solution)/shard_map/pallas_call | solution.py:547

commit v8 on v7

--- a/solution.py
+++ b/solution.py
@@ -452,14 +452,15 @@
     for i, (phase, j, a) in enumerate(pieces):
         times.append((6.15 + 0.7 * i, step_pair_in, i))
         if a == 0:
-            at = 6.9 + 0.7 * i if phase == 0 else (12.6 if j == 0 else 14.0)
+            at = 6.9 + 0.7 * i if phase == 0 else (11.2 if j == 0 else 14.0)
             times.append((at, step_far_in, i))
-        times.append((8.75 + 0.7 * i + phase, step_outer_in, i))
+        late = 1.0 if phase == 1 else (0.3 if (j, a) == (mine - 1, 1) else 0.0)
+        times.append((8.75 + 0.7 * i + late, step_outer_in, i))
     for j in heads:
         times.append((7.55 + 2.8 * j, step_own_halo, j))
         times.append((11.06 + 1.42 * j, step_forward_pair, j))
         times.append((11.35 + 1.8 * j, step_forward_own, j))
-        times.append((15.0 + 1.5 * j, step_backward_pair, j))
+        times.append((14.9 + 1.55 * j, step_backward_pair, j))
         times.append((16.6 + (4.5 + 0.5 * j if j > 0 else 0.0), step_backward_own, j))
     for _, step, index in sorted(times, key=lambda entry: entry[0]):
         step(index)

time: 26.2 us -> 25.5 us (0.973)
  Pallas kernels: 25.5 us -> 24.7 us
    pallas_call x1, Pallas kernels: 24.5 us -> 23.8 us  [on_device(): pl.pallas_call(functools.partial(kernel, sizes), out_shape=[jax.ShapeDtyp...]
where the time goes in v8:
time: 25.5 us; the launch traced here: 25.4 us
  Pallas kernels  24.7 us (97%)
  between operations  0.64 us (3%)
    pallas_call x1, Pallas kernels, on_device(): pl.pallas_call(functools.partial(kernel, sizes), out_shape=[jax.ShapeDtyp...  23.8 us
    pallas_call x1, Pallas kernels, on_device(): pl.pallas_call(put_out, out_shape=[jax.ShapeDtypeStruct(flat, low)] * 4,...  0.91 us

profile of v8, /device:TPU:0, one launch (start us, length us, event | category | flops | bytes accessed | tf_op | source)
XLA Modules:
  0.0 25.4 jit_solution(1719240113648213861)
XLA Ops:
  0.6 23.8 %shard_map.84 = (bf16[128,768]{1,0:T(8,128)(2,1)S(1)}, bf16[128,768]{1,0:T(8,128)(2,1)S(1)}, bf16[128,768]{1,0:T(8,128)(2,1)S(1)}, bf16[128,768]{1,0:T(8,128)(2,1)S(1)}) custom-call(s32[2,6]{1,0:T(2,128)} %win_hbm.1, bf16[128,768]{1,0:T(8,128)(2,1)} %bitcast.8, bf16[128,768]{1,0:T(8,128)(2,1)} %bitcast.9, bf16[128,768]{1,0:T(8,128)(2,1)} %bitcast.10, ...), custom_call_target="tpu_custom_call" | custom-call | tf_op jit(solution)/shard_map/pallas_call | solution.py:512
  24.5 0.9 %shard_map.85 = (bf16[128,768]{1,0:T(8,128)(2,1)}, bf16[128,768]{1,0:T(8,128)(2,1)}, bf16[128,768]{1,0:T(8,128)(2,1)}, bf16[128,768]{1,0:T(8,128)(2,1)}) custom-call(bf16[128,768]{1,0:T(8,128)(2,1)S(1)} %get-tuple-element.12.refs_0_, bf16[128,768]{1,0:T(8,128)(2,1)S(1)} %get-tuple-element.13.refs_1_, bf16[128,768]{1,0:T(8,128)(2,1)S(1)} %get-tuple-element.14.refs_2_, ...), custom_call_target="tpu_custom_call" | custom-call | tf_op jit(solution)/shard_map/pallas_call | solution.py:548

commit v9 on v8

--- a/solution.py
+++ b/solution.py
@@ -130,13 +130,25 @@
             device_id_type=MESH,
         )
 
+    def piece_sem(i):
+        phase, j, _ = pieces[i]
+        return i if phase == 0 else 2 * mine + j
+
+    def arrive_piece(i, slot, sem):
+        phase, j, a = pieces[i]
+        rows = near.at[phase, j, slice(a, a + 1) if phase == 0 else slice(0, 2), slot, 0:tokens, :]
+        pltpu.make_async_copy(rows, rows, sem.at[piece_sem(i)]).wait()
+
+    def group(i):
+        return (i,) if pieces[i][0] == 0 else (i - 1, i)
+
     def to_pair(i):
         phase, j, a = pieces[i]
         return remote(
             ins[phase][a].at[:, head_cols(j, True)],
             main_rows(i, PAIR),
             send_sem.at[TO_PAIR],
-            pair_sem.at[i],
+            pair_sem.at[piece_sem(i)],
             (pair, sp),
         )
 
@@ -155,7 +167,7 @@
             main_rows(i, PAIR),
             main_rows(i, OUTER),
             send_sem.at[TO_OUTER],
-            outer_sem.at[i],
+            outer_sem.at[piece_sem(i)],
             (inner_to, sp),
         )
 
@@ -383,9 +395,10 @@
         ]
 
     def step_pair_in(i):
-        to_pair(i).wait_recv()
-        when(has_far, lambda: pair_to_outer(i).start())
-        halos(i, PAIR)
+        arrive_piece(i, PAIR, pair_sem)
+        for at in group(i):
+            when(has_far, lambda: pair_to_outer(at).start())
+            halos(at, PAIR)
 
     def step_far_in(i):
         phase, j, _ = pieces[i]
@@ -400,8 +413,9 @@
     def step_outer_in(i):
         @pl.when(has_outer)
         def _():
-            pair_to_outer(i).wait_recv()
-            halos(i, OUTER)
+            arrive_piece(i, OUTER, outer_sem)
+            for at in group(i):
+                halos(at, OUTER)
 
     def arrived(ref, sem):
         pltpu.make_async_copy(ref, ref, sem).wait()
@@ -450,12 +464,15 @@
 
     times = [(0.0, step_own_out, 0), (7.5, step_own_out, 1)]
     for i, (phase, j, a) in enumerate(pieces):
-        times.append((6.15 + 0.7 * i, step_pair_in, i))
+        alone = phase == 0 or a == 1
+        if alone:
+            times.append((6.15 + 0.7 * i, step_pair_in, i))
         if a == 0:
             at = 6.9 + 0.7 * i if phase == 0 else (11.2 if j == 0 else 14.0)
             times.append((at, step_far_in, i))
-        late = 1.0 if phase == 1 else (0.3 if (j, a) == (mine - 1, 1) else 0.0)
-        times.append((8.75 + 0.7 * i + late, step_outer_in, i))
+        late = 1.0 if phase == 1 else (0.95 - 0.65 * a if j == mine - 1 else 0.0)
+        if alone:
+            times.append((8.75 + 0.7 * i + late, step_outer_in, i))
     for j in heads:
         times.append((7.55 + 2.8 * j, step_own_halo, j))
         times.append((11.06 + 1.42 * j, step_forward_pair, j))
@@ -528,8 +545,8 @@
             pltpu.VMEM((4, 8, tokens), jnp.float32),
             pltpu.SemaphoreType.DMA((3,)),
             pltpu.SemaphoreType.DMA((STAT + 8,)),
-            pltpu.SemaphoreType.DMA((4 * mine,)),
-            pltpu.SemaphoreType.DMA((4 * mine,)),
+            pltpu.SemaphoreType.DMA((3 * mine,)),
+            pltpu.SemaphoreType.DMA((3 * mine,)),
             pltpu.SemaphoreType.DMA((2, mine)),
             pltpu.SemaphoreType.DMA((2, mine, 2)),
             pltpu.SemaphoreType.DMA((mine, 2)),

time: 25.5 us -> 25.7 us (level); the launches traced: 25.4 us -> 25.3 us
  no operation moved by 1% of the time
where the time goes in v9:
time: 25.7 us; the launch traced here: 25.3 us
  Pallas kernels  24.7 us (96%)
  between operations  0.64 us (2%)
    pallas_call x1, Pallas kernels, on_device(): pl.pallas_call(functools.partial(kernel, sizes), out_shape=[jax.ShapeDtyp...  23.7 us
    pallas_call x1, Pallas kernels, on_device(): pl.pallas_call(put_out, out_shape=[jax.ShapeDtypeStruct(flat, low)] * 4,...  0.91 us

profile of v9, /device:TPU:0, one launch (start us, length us, event | category | flops | bytes accessed | tf_op | source)
XLA Modules:
  0.0 25.3 jit_solution(7472824179918857661)
XLA Ops:
  0.6 23.7 %shard_map.84 = (bf16[128,768]{1,0:T(8,128)(2,1)S(1)}, bf16[128,768]{1,0:T(8,128)(2,1)S(1)}, bf16[128,768]{1,0:T(8,128)(2,1)S(1)}, bf16[128,768]{1,0:T(8,128)(2,1)S(1)}) custom-call(s32[2,6]{1,0:T(2,128)} %win_hbm.1, bf16[128,768]{1,0:T(8,128)(2,1)} %bitcast.8, bf16[128,768]{1,0:T(8,128)(2,1)} %bitcast.9, bf16[128,768]{1,0:T(8,128)(2,1)} %bitcast.10, ...), custom_call_target="tpu_custom_call" | custom-call | tf_op jit(solution)/shard_map/pallas_call | solution.py:529
  24.4 0.9 %shard_map.85 = (bf16[128,768]{1,0:T(8,128)(2,1)}, bf16[128,768]{1,0:T(8,128)(2,1)}, bf16[128,768]{1,0:T(8,128)(2,1)}, bf16[128,768]{1,0:T(8,128)(2,1)}) custom-call(bf16[128,768]{1,0:T(8,128)(2,1)S(1)} %get-tuple-element.12.refs_0_, bf16[128,768]{1,0:T(8,128)(2,1)S(1)} %get-tuple-element.13.refs_1_, bf16[128,768]{1,0:T(8,128)(2,1)S(1)} %get-tuple-element.14.refs_2_, ...), custom_call_target="tpu_custom_call" | custom-call | tf_op jit(solution)/shard_map/pallas_call | solution.py:565

commit v10 on v8

--- a/solution.py
+++ b/solution.py
@@ -303,9 +303,14 @@
             (pair, sp),
         )
 
+    def score(j, frame):
+        at = slice((frame - OWN) * tokens, (frame - OWN + 1) * tokens)
+        scores_ref[at] = dot_nt(near[1, j, 0, frame, 0:tokens, :], around(0, j, 0, frame))
+
     def forward(j, frame):
         at = slice((frame - OWN) * tokens, (frame - OWN + 1) * tokens)
-        scores_ref[at] = dot_nt(near[1, j, 0, frame, 0:tokens, :], around(0, j, 0, frame))
+        if frame == OWN:
+            score(j, frame)
         grad_weights_ref[at] = dot_nt(near[1, j, 1, frame, 0:tokens, :], around(0, j, 1, frame))
         scores = scores_ref[at] * scale2 + window(j, frame)
         top = jnp.max(scores, axis=1, keepdims=True)
@@ -415,8 +420,11 @@
 
     columns = {}
 
+    def step_score_pair(j):
+        arrive_halos(0, j, False)
+        score(j, PAIR)
+
     def step_forward_pair(j):
-        arrive_halos(0, j, False)
         forward(j, PAIR)
         for kind in (0, 1):
             give(kind, j).start()
@@ -458,6 +466,7 @@
         times.append((8.75 + 0.7 * i + late, step_outer_in, i))
     for j in heads:
         times.append((7.55 + 2.8 * j, step_own_halo, j))
+        times.append((10.36 + 1.4 * j, step_score_pair, j))
         times.append((11.06 + 1.42 * j, step_forward_pair, j))
         times.append((11.35 + 1.8 * j, step_forward_own, j))
         times.append((14.9 + 1.55 * j, step_backward_pair, j))

time: 25.5 us -> 25.8 us (1.012)
  Pallas kernels: 24.7 us -> 25 us
where the time goes in v10:
time: 25.8 us; the launch traced here: 25.6 us
  Pallas kernels  25 us (97%)
  between operations  0.64 us (2%)
    pallas_call x1, Pallas kernels, on_device(): pl.pallas_call(functools.partial(kernel, sizes), out_shape=[jax.ShapeDtyp...  24.1 us
    pallas_call x1, Pallas kernels, on_device(): pl.pallas_call(put_out, out_shape=[jax.ShapeDtypeStruct(flat, low)] * 4,...  0.91 us

profile of v10, /device:TPU:0, one launch (start us, length us, event | category | flops | bytes accessed | tf_op | source)
XLA Modules:
  0.0 25.6 jit_solution(8470524220146209709)
XLA Ops:
  0.6 24.1 %shard_map.84 = (bf16[128,768]{1,0:T(8,128)(2,1)S(1)}, bf16[128,768]{1,0:T(8,128)(2,1)S(1)}, bf16[128,768]{1,0:T(8,128)(2,1)S(1)}, bf16[128,768]{1,0:T(8,128)(2,1)S(1)}) custom-call(s32[2,6]{1,0:T(2,128)} %win_hbm.1, bf16[128,768]{1,0:T(8,128)(2,1)} %bitcast.8, bf16[128,768]{1,0:T(8,128)(2,1)} %bitcast.9, bf16[128,768]{1,0:T(8,128)(2,1)} %bitcast.10, ...), custom_call_target="tpu_custom_call" | custom-call | tf_op jit(solution)/shard_map/pallas_call | solution.py:521
  24.7 0.9 %shard_map.85 = (bf16[128,768]{1,0:T(8,128)(2,1)}, bf16[128,768]{1,0:T(8,128)(2,1)}, bf16[128,768]{1,0:T(8,128)(2,1)}, bf16[128,768]{1,0:T(8,128)(2,1)}) custom-call(bf16[128,768]{1,0:T(8,128)(2,1)S(1)} %get-tuple-element.12.refs_0_, bf16[128,768]{1,0:T(8,128)(2,1)S(1)} %get-tuple-element.13.refs_1_, bf16[128,768]{1,0:T(8,128)(2,1)S(1)} %get-tuple-element.14.refs_2_, ...), custom_call_target="tpu_custom_call" | custom-call | tf_op jit(solution)/shard_map/pallas_call | solution.py:557

commit v11 on v8

--- a/solution.py
+++ b/solution.py
@@ -454,7 +454,9 @@
         if a == 0:
             at = 6.9 + 0.7 * i if phase == 0 else (11.2 if j == 0 else 14.0)
             times.append((at, step_far_in, i))
-        late = 1.0 if phase == 1 else (0.3 if (j, a) == (mine - 1, 1) else 0.0)
+        late = 0.3 if (j, a) == (mine - 1, 1) else 0.0
+        if phase == 1:
+            late = 2.2 if 0 < j < mine - 1 else 1.0
         times.append((8.75 + 0.7 * i + late, step_outer_in, i))
     for j in heads:
         times.append((7.55 + 2.8 * j, step_own_halo, j))

time: 25.5 us -> 25.5 us (level)
  no operation moved by 1% of the time
where the time goes in v11:
time: 25.5 us; the launch traced here: 25.4 us
  Pallas kernels  24.7 us (97%)
  between operations  0.64 us (3%)
    pallas_call x1, Pallas kernels, on_device(): pl.pallas_call(functools.partial(kernel, sizes), out_shape=[jax.ShapeDtyp...  23.8 us
    pallas_call x1, Pallas kernels, on_device(): pl.pallas_call(put_out, out_shape=[jax.ShapeDtypeStruct(flat, low)] * 4,...  0.91 us

profile of v11, /device:TPU:0, one launch (start us, length us, event | category | flops | bytes accessed | tf_op | source)
XLA Modules:
  0.0 25.4 jit_solution(16752888722145467887)
XLA Ops:
  0.6 23.8 %shard_map.84 = (bf16[128,768]{1,0:T(8,128)(2,1)S(1)}, bf16[128,768]{1,0:T(8,128)(2,1)S(1)}, bf16[128,768]{1,0:T(8,128)(2,1)S(1)}, bf16[128,768]{1,0:T(8,128)(2,1)S(1)}) custom-call(s32[2,6]{1,0:T(2,128)} %win_hbm.1, bf16[128,768]{1,0:T(8,128)(2,1)} %bitcast.8, bf16[128,768]{1,0:T(8,128)(2,1)} %bitcast.9, bf16[128,768]{1,0:T(8,128)(2,1)} %bitcast.10, ...), custom_call_target="tpu_custom_call" | custom-call | tf_op jit(solution)/shard_map/pallas_call | solution.py:514
  24.5 0.9 %shard_map.85 = (bf16[128,768]{1,0:T(8,128)(2,1)}, bf16[128,768]{1,0:T(8,128)(2,1)}, bf16[128,768]{1,0:T(8,128)(2,1)}, bf16[128,768]{1,0:T(8,128)(2,1)}) custom-call(bf16[128,768]{1,0:T(8,128)(2,1)S(1)} %get-tuple-element.12.refs_0_, bf16[128,768]{1,0:T(8,128)(2,1)S(1)} %get-tuple-element.13.refs_1_, bf16[128,768]{1,0:T(8,128)(2,1)S(1)} %get-tuple-element.14.refs_2_, ...), custom_call_target="tpu_custom_call" | custom-call | tf_op jit(solution)/shard_map/pallas_call | solution.py:550
